TPU v7x, 128 devices: a whole 4x4x4 slice. The times are simulated.
128 devices in a mesh: comp: 16 (over y, x), space: 8 (over z, core).
Axes of the slice: x: 4, y: 4, z: 4, core: 2. Of those that a mesh axis runs over, the one named last changes fastest.
Arguments:
- spectrum: float32 [1296, 512, 256], P('comp', 'space'), may hold values from 0.05 to 2
- mask: int32 [512, 256], P('space'), may hold values 0 or 1
- depth_level: int32 [512, 256], P('space'), may hold values from 0 to 7
- speed_table: float32 [36, 8], replicated, may hold values from 0.2 to 1.8
- wind_u: float32 [512, 256], P('space'), may hold values from -4 to 4
- wind_v: float32 [512, 256], P('space'), may hold values from -4 to 4
- substeps: int32 [512], P('space'), may hold values from 1 to 4, as said below
- coupling: bfloat16 [1296, 1296], replicated, may hold values from -0.15625 to 0.15625
Outputs:
- spectrum_next: float32 [1296, 512, 256], P('comp', 'space')
Inputs may be any that keep to these rules, and one draw needn't show every extreme that they name: `substeps`: every strip of 64 consecutive rows holds a run of 8 consecutive rows with 4 turns.
All inputs are finite; a program needn't handle non-finite values. No bound on the sum of `mask` on one device may be relied on, other than what follows from the above.
Results may differ from a plain program's by a relative error of at most 0.0011.
Values sent between devices are 32-bit elements; how exact they have to be, the bound alone decides.
No kernel may reach another device: no remote copies, remote signals or barrier semaphores. Data moves between devices by JAX's collectives and lax.ppermute only.
A program may use at most 128 MiB of HBM per device.

v0:
```python
import math

import jax
import jax.numpy as jnp
from jax import lax
from jax.sharding import PartitionSpec as P

NF = 36
ND = 36
LEVELS = 8


TIME_STEP = 1.0
WIND_RATE = 0.3
BREAK_RATE = 0.8
MIXING = 0.5


def with_halo(cells, sides, width):
    for axis, dim in sides:
        count = lax.axis_size(axis)
        ends = count - 1
        head = lax.slice_in_dim(cells, 0, width, axis=dim)
        tail = lax.slice_in_dim(cells, cells.shape[dim] - width, cells.shape[dim], axis=dim)
        cells = jnp.concatenate(
            [
                lax.ppermute(tail, axis, [(i, (i + 1) % count) for i in range(ends)]),
                cells,
                lax.ppermute(head, axis, [((i + 1) % count, i) for i in range(ends)]),
            ],
            axis=dim,
        )
    return cells


def spectral_tables(component_index):
    frequency = component_index // ND
    direction = component_index % ND
    direction_angle = 2.0 * math.pi / ND * (direction.astype(jnp.float32) + 0.5)
    freq_value = frequency.astype(jnp.float32)
    phase_speed = 1.5 * jnp.power(1.1, -freq_value)
    norm_total = ND * jnp.sum(jnp.power(1.1, 2.0 * jnp.arange(NF).astype(jnp.float32)))
    weight = jnp.power(1.1, 2.0 * freq_value) / norm_total
    damping = BREAK_RATE * (freq_value + 1.0) / NF
    return (jnp.cos(direction_angle), jnp.sin(direction_angle), phase_speed, weight, damping)


def upwind_sweep(padded, courant, grid_dim):
    extent = courant.shape[grid_dim]

    def window_at(offset):
        return lax.slice_in_dim(padded, offset, offset + extent, axis=grid_dim)

    centre = window_at(2)
    forward = courant >= 0.0
    upwind_near = jnp.where(forward, window_at(1), window_at(3))
    upwind_far = jnp.where(forward, window_at(0), window_at(4))
    magnitude = jnp.abs(courant)
    return (
        centre
        - 0.5 * magnitude * (3.0 * centre - 4.0 * upwind_near + upwind_far)
        + 0.5 * magnitude * magnitude * (centre - 2.0 * upwind_near + upwind_far)
    )


def source_row(wave_field, east_wind, north_wind, turns, coupling, tables):
    cos_part, sin_part, phase_speed, weight, damping = tables
    rate_in = WIND_RATE * jnp.maximum(
        0.0,
        east_wind[None, :] * cos_part[:, None]
        + north_wind[None, :] * sin_part[:, None]
        - phase_speed[:, None],
    )
    step_size = TIME_STEP / turns.astype(jnp.float32)

    def advance(repeat, current):
        steepness = jnp.sum(weight[:, None] * current, axis=0)
        dissipation = damping[:, None] * (steepness * steepness)[None, :]
        interaction = jnp.dot(
            coupling, current.astype(jnp.bfloat16), preferred_element_type=jnp.float32
        )
        return current + step_size * ((rate_in - dissipation) * current + MIXING * interaction)

    return lax.fori_loop(0, turns, advance, wave_field)


def courant_base(component_index, level_hot, speed_table):
    freq_hot = (
        (component_index // ND)[:, None] == jnp.arange(NF, dtype=jnp.int32)[None, :]
    ).astype(jnp.float32)
    rows_table = jnp.dot(freq_hot, speed_table, precision=lax.Precision.HIGHEST)
    return jnp.einsum("cl,lxy->cxy", rows_table, level_hot, precision=lax.Precision.HIGHEST)


def level_table(depth_rows):
    return (depth_rows[None] == jnp.arange(LEVELS, dtype=jnp.int32)[:, None, None]).astype(
        jnp.float32
    )


def on_device(spectrum, mask, depth_level, speed_table, wind_u, wind_v, substeps, coupling):
    groups = lax.axis_size("comp")
    per_group = spectrum.shape[0]
    strip_rows = spectrum.shape[1]
    columns = spectrum.shape[2]
    own_rows = strip_rows // groups
    group_index = lax.axis_index("comp")
    sea_mask = mask.astype(jnp.float32)
    own_components = group_index * per_group + jnp.arange(per_group, dtype=jnp.int32)
    everyone = jnp.arange(groups * per_group, dtype=jnp.int32)
    tables_own = spectral_tables(own_components)
    tables_all = spectral_tables(everyone)
    base_own = courant_base(own_components, level_table(depth_level), speed_table)
    wave_field = spectrum * sea_mask[None]
    padded = with_halo(wave_field, (("space", 1),), 2)
    wave_field = upwind_sweep(padded, base_own * tables_own[0][:, None, None], 1) * sea_mask[None]
    padded_cross = jnp.pad(wave_field, ((0, 0), (0, 0), (2, 2)))
    wave_field = (
        upwind_sweep(padded_cross, base_own * tables_own[1][:, None, None], 2) * sea_mask[None]
    )
    shaped = wave_field.reshape(per_group, groups, own_rows, columns)
    gathered = lax.all_to_all(shaped, "comp", split_axis=1, concat_axis=0, tiled=True)
    spectra = gathered.reshape(groups * per_group, own_rows, columns)

    def own_slice(source_array):
        return lax.dynamic_slice_in_dim(source_array, group_index * own_rows, own_rows, 0)

    east_rows = own_slice(wind_u)
    north_rows = own_slice(wind_v)
    turn_rows = own_slice(substeps)
    results = []
    for row_index in range(own_rows):
        results.append(
            source_row(
                spectra[:, row_index],
                east_rows[row_index],
                north_rows[row_index],
                turn_rows[row_index],
                coupling,
                tables_all,
            )
        )
    updated = jnp.stack(results, axis=1)
    returned = lax.all_to_all(
        updated.reshape(groups * per_group, 1, own_rows, columns),
        "comp",
        split_axis=0,
        concat_axis=1,
        tiled=True,
    )
    return returned.reshape(per_group, strip_rows, columns)


def solution(mesh):
    placed = (
        P("comp", "space", None),
        P("space", None),
        P("space", None),
        P(),
        P("space", None),
        P("space", None),
        P("space"),
        P(),
    )
    return jax.shard_map(
        on_device, mesh=mesh, in_specs=placed, out_specs=P("comp", "space", None), check_vma=False
    )
```

profile of v0, /device:TPU:32, one launch (start us, length us, event | category | flops | bytes accessed | tf_op | source)
XLA Modules:
  0.0 314.2 jit_solution(11082087586747197452)
XLA Ops:
  0.0 0.9 convert_element_type.91
  0.9 5.6 %copy_multiply_fusion = f32[81,64,256]{2,0,1:T(8,128)S(1)} fusion(f32[81,64,256]{2,1,0:T(8,128)} %param.16, f32[64,256]{1,0:T(8,128)S(1)} %convert_element_type.91), kind=kLoop, calls=%fused_computation.112 | loop fusion | flops 1327104 | bytes 10682368 | tf_op jit(solution)/shard_map/mul | solution.py:114
  6.5 2.4 copy-done.2
  9.0 1.9 collective-permute-start.1
  10.9 2.4 collective-permute-start
  13.3 0.1 fusion.97
  13.4 0.2 convolution_bitcast_fusion
  13.6 0.3 collective-permute-done.1
  13.9 3.8 %collective-permute-done = f32[81,2,256]{2,0,1:T(8,128)S(1)} collective-permute-done((f32[81,2,256]{2,0,1:T(8,128)S(1)}, f32[81,2,256]{2,0,1:T(8,128)S(1)}, u32[]{:S(2)}, u32[]{:S(2)}) %collective-permute-start) | collective-permute-done | bytes 165920 | tf_op jit(solution)/shard_map/ppermute | solution.py:27
  17.7 17.9 %fusion.65 = (f32[81,64,256]{2,0,1:T(8,128)}, f32[81,64,256]{2,0,1:T(8,128)}) fusion(f32[81,64,256]{2,0,1:T(8,128)} %copy-done.2, f32[81,2,256]{2,0,1:T(8,128)S(1)} %collective-permute-done.1, f32[81,2,256]{2,0,1:T(8,128)S(1)} %collective-permute-done, f32[81]{0:T(128)S(1)} %get-tuple-element.422, f32[64,256]{1,0:T(8,128)S(1)} %convert_element_type.91, ...), kind=kOutput, calls=%fused_computation.101 | convolution fusion | flops 158056448 | bytes 16391012 | tf_op jit(solution)/shard_map/cl,lxy->cxy/dot_general | solution.py:92
  35.7 17.8 %fusion.69 = f32[81,64,256]{2,0,1:T(8,128)} fusion(f32[81,64,256]{2,0,1:T(8,128)} %get-tuple-element.419, f32[81,64,256]{2,0,1:T(8,128)} %get-tuple-element.420, f32[81]{0:T(128)S(1)} %get-tuple-element.421, f32[64,256]{1,0:T(8,128)S(1)} %convert_element_type.91), kind=kLoop, calls=%fused_computation.105 | loop fusion | flops 25214976 | bytes 15991108 | tf_op jit(solution)/shard_map/mul | solution.py:119
  53.5 7.1 %copy.20 = f32[81,16,4,256]{3,2,0,1:T(4,128)} copy(f32[81,16,4,256]{3,0,2,1:T(8,128)} %bitcast.57) | data formatting | bytes 10616832 | tf_op jit(solution)/shard_map/reshape | solution.py:121
  60.5 7.2 %all-to-all-start = ((f32[81,16,4,256]{3,2,0,1:T(4,128)}), f32[81,16,4,256]{3,2,0,1:T(4,128)}, u32[]{:S(2)}, u32[]{:S(2)}) async-start(f32[81,16,4,256]{3,2,0,1:T(4,128)} %copy.20), calls=%async_computation | async-start | bytes 10616832 | tf_op jit(solution)/shard_map/all_to_all | solution.py:122
  67.8 0.1 dynamic_slice.9
  67.8 0.7 fusion.101
  71.1 0.6 power_reduce_fusion
  72.3 0.1 fusion.91
  72.4 1.0 constant_dynamic-slice_fusion.4
  73.4 0.1 fusion.86
  73.4 73.1 %all-to-all-done = f32[81,16,4,256]{3,2,0,1:T(4,128)} async-done(((f32[81,16,4,256]{3,2,0,1:T(4,128)}), f32[81,16,4,256]{3,2,0,1:T(4,128)}, u32[]{:S(2)}, u32[]{:S(2)}) %all-to-all-start) | async-done | bytes 5308448 | tf_op jit(solution)/shard_map/all_to_all | solution.py:122
  146.6 14.2 %fusion.100 = (f32[1296,1,256]{2,1,0:T(1,128)}, f32[1296,1,256]{2,1,0:T(1,128)S(1)}, f32[1296,1,256]{2,1,0:T(1,128)}, f32[1296,1,256]{2,1,0:T(1,128)}) fusion(f32[1296,4,256]{2,1,0:T(4,128)} %bitcast.4), kind=kLoop, calls=%fused_computation.163 | loop fusion | bytes 10616832 | tf_op jit(solution)/shard_map/slice | solution.py:135
  160.8 0.1 copy.31
  160.8 4.9 %while.47 = (s32[]{:T(128)}, f32[1296,256]{1,0:T(8,128)S(1)}, s32[]{:T(128)}, f32[]{:T(128)}, bf16[1296,1296]{1,0:T(8,128)(2,1)}, /*index=5*/f32[]{:T(128)}, f32...) while((s32[]{:T(128)}, f32[1296,256]{1,0:T(8,128)S(1)}, ...), condition=%wide.region_12.13_spmd.clone, body=%wide.region_10.12_spmd.clone.sunk | while | flops 865300352 | bytes 23475288 | solution.py:84
  161.5 0.1 copy.67
  161.7 0.3 multiply_reduce_fusion.11
  161.9 1.6 copy-done.8
  163.6 1.5 fusion.131
  165.8 1.0 stack.18
  166.7 0.3 copy-done.7
  167.1 0.1 copy.32
  167.2 4.8 %while.46 = (s32[]{:T(128)}, f32[1296,256]{1,0:T(8,128)S(1)}, s32[]{:T(128)}, f32[]{:T(128)}, bf16[1296,1296]{1,0:T(8,128)(2,1)}, /*index=5*/f32[]{:T(128)}, f32...) while((s32[]{:T(128)}, f32[1296,256]{1,0:T(8,128)S(1)}, ...), condition=%wide.region_9.10_spmd.clone, body=%wide.region_7.9_spmd.clone.sunk | while | flops 865300352 | bytes 23475288 | solution.py:84
  167.8 0.1 copy.66
  167.9 0.3 multiply_reduce_fusion.10
  168.2 1.6 copy-done.9
  169.9 1.5 fusion.128
  172.0 1.8 stack.17
  173.8 0.1 copy.33
  173.9 8.8 %while.45 = (s32[]{:T(128)}, f32[1296,256]{1,0:T(8,128)S(1)}, s32[]{:T(128)}, f32[]{:T(128)}, bf16[1296,1296]{1,0:T(8,128)(2,1)}, /*index=5*/f32[]{:T(128)}, f32...) while((s32[]{:T(128)}, f32[1296,256]{1,0:T(8,128)S(1)}, ...), condition=%wide.region_6.7_spmd.clone, body=%wide.region_4.6_spmd.clone.sunk | while | flops 865300352 | bytes 23475288 | solution.py:84
  174.5 0.1 copy.65
  174.6 0.3 multiply_reduce_fusion.9
  174.9 1.6 copy-done.10
  176.5 1.5 fusion.125
  178.6 0.1 copy.65
  178.7 0.3 multiply_reduce_fusion.9
  179.0 1.6 copy-done.10
  180.7 1.5 fusion.125
  182.7 1.8 stack.16
  184.6 0.1 copy.34
  184.7 9.0 %while.44 = (s32[]{:T(128)}, f32[1296,256]{1,0:T(8,128)S(1)}, s32[]{:T(128)}, f32[]{:T(128)}, bf16[1296,1296]{1,0:T(8,128)(2,1)}, /*index=5*/f32[]{:T(128)}, f32...) while((s32[]{:T(128)}, f32[1296,256]{1,0:T(8,128)S(1)}, ...), condition=%wide.region_3.4_spmd.clone, body=%wide.region_1.3_spmd.clone.sunk | while | flops 865300352 | bytes 23475288 | solution.py:84
  185.2 0.1 copy.64
  185.3 0.3 multiply_reduce_fusion.8
  185.6 1.6 copy-done.11
  187.2 1.5 fusion.122
  189.3 0.1 copy.64
  189.4 0.3 multiply_reduce_fusion.8
  189.7 1.6 copy-done.11
  191.4 1.5 fusion.122
  193.7 1.0 stack.15
  194.6 0.3 copy-done.4
  195.0 0.4 copy-done.6
  195.4 5.1 %maximum_bitcast_fusion = f32[1296,1,4,256]{3,2,1,0:T(4,128)S(1)} fusion(f32[1296,1,256]{2,1,0:T(1,128)S(1)} %stack.18, f32[1296,1,256]{2,1,0:T(1,128)S(1)} %copy-done.4, f32[1296,1,256]{2,1,0:T(1,128)S(1)} %copy-done.6, f32[1296,1,256]{2,1,0:T(1,128)S(1)} %stack.15), kind=kLoop, calls=%fused_computation.113 | loop fusion | flops 3981312 | bytes 10616832 | tf_op jit(solution)/shard_map/reshape | solution.py:145
  200.4 102.6 %all_to_all.30 = f32[1296,1,4,256]{3,2,1,0:T(4,128)S(1)} all-to-all(f32[1296,1,4,256]{3,2,1,0:T(4,128)S(1)} %maximum_bitcast_fusion), channel_id=1, replica_groups=mesh['comp'=16,'space'=8] {'comp'}, dimensions={0} | all-to-all | bytes 10616832 | tf_op jit(solution)/shard_map/all_to_all | solution.py:144
  303.0 3.9 %copy.21 = f32[81,16,1,4,256]{4,3,1,0,2:T(4,128)} copy(f32[81,16,1,4,256]{4,3,0,1,2:T(4,128)S(1)} %bitcast.58) | data formatting | bytes 10616832 | tf_op jit(solution)/shard_map/all_to_all | solution.py:144
  306.9 7.3 %reshape.99 = f32[81,64,256]{2,1,0:T(8,128)} reshape(f32[81,16,1,4,256]{4,3,1,0,2:T(4,128)} %copy.21) | data formatting | bytes 10616832 | tf_op jit(solution)/shard_map/reshape | solution.py:151
  (42 shorter events, 0.3 us)
Async XLA Ops:
  0.0 13.4 %copy-start = (f32[36,8]{0,1:T(8,128)S(1)}, f32[36,8]{0,1:T(8,128)}, u32[]{:S(2)}) copy-start(f32[36,8]{0,1:T(8,128)} %param.19) | copy-start | bytes 3460
  0.9 16.9 %copy-start.12 = (s32[64,256]{1,0:T(8,128)S(1)}, s32[64,256]{1,0:T(8,128)}, u32[]{:S(2)}) copy-start(s32[64,256]{1,0:T(8,128)} %param.18) | copy-start | bytes 196612
  6.5 2.5 copy-start.2
  9.0 4.9 %collective-permute-start.1 = (f32[81,2,256]{2,0,1:T(8,128)S(1)}, f32[81,2,256]{2,0,1:T(8,128)S(1)}, u32[]{:S(2)}, u32[]{:S(2)}) collective-permute-start(f32[81,2,256]{2,0,1:T(8,128)S(1)} %get-tuple-element.402), channel_id=1, source_target_pairs={{1,0},{2,1},{3,2},{4,3},{5,4},{6,5},{7,6},{9,8},{10,9},{11,10},{12... | collective-permute-start | bytes 497672 | tf_op jit(solution)/shard_map/ppermute | solution.py:29
  10.9 6.8 %collective-permute-start = (f32[81,2,256]{2,0,1:T(8,128)S(1)}, f32[81,2,256]{2,0,1:T(8,128)S(1)}, u32[]{:S(2)}, u32[]{:S(2)}) collective-permute-start(f32[81,2,256]{2,0,1:T(8,128)S(1)} %get-tuple-element.401), channel_id=1, source_target_pairs={{0,1},{1,2},{2,3},{3,4},{4,5},{5,6},{6,7},{8,9},{9,10},{10,11},{11... | collective-permute-start | bytes 497672 | tf_op jit(solution)/shard_map/ppermute | solution.py:27
  60.5 7.2 %copy-start.13 = (s32[64]{0:T(128)S(1)}, s32[64]{0:T(128)}, u32[]{:S(2)}) copy-start(s32[64]{0:T(128)} %param.22) | copy-start | bytes 772
  60.5 86.1 %all-to-all-start = ((f32[81,16,4,256]{3,2,0,1:T(4,128)}), f32[81,16,4,256]{3,2,0,1:T(4,128)}, u32[]{:S(2)}, u32[]{:S(2)}) async-start(f32[81,16,4,256]{3,2,0,1:T(4,128)} %copy.20), calls=%async_computation | async-start | bytes 10616832 | tf_op jit(solution)/shard_map/all_to_all | solution.py:122
  161.5 2.0 copy-start.8
  165.8 1.3 copy-start.7
  167.8 2.0 copy-start.9
  172.0 1.8 copy-start.5
  174.5 2.0 copy-start.10
  178.6 2.0 copy-start.10
  182.7 1.8 copy-start.3
  185.2 2.0 copy-start.11
  189.3 2.0 copy-start.11
  193.6 1.3 copy-start.4
  193.6 1.7 copy-start.6
  306.9 7.3 %copy-start.1 = (f32[36,8]{0,1:T(8,128)S(1)}, f32[36,8]{0,1:T(8,128)}, u32[]{:S(2)}) copy-start(f32[36,8]{0,1:T(8,128)} %param.19) | copy-start | bytes 3460
where the time goes:
time: 316 us; the launch traced here: 314 us
  blocking collectives  103 us (33%)
  waiting for transfers between devices  77.3 us (24%)
  local copies, waits for them, and re-layouts  53.9 us (17%)
  other arithmetic  31.9 us (10%)
  matrix products  27.1 us (9%)
  starting transfers between devices  11.5 us (4%)
  loops' own time  6.47 us (2%)
  between operations  3.42 us (1%)
    all_to_all x1, blocking collectives, on_device(): lax.all_to_all(updated.reshape(groups * per_group, 1, own_rows, columns),...  103 us
    all_to_all x1, waiting for transfers between devices, on_device(): lax.all_to_all(shaped, 'comp', split_axis=1, concat_axis=0, tiled=True)  73.1 us
    dot_general x1, matrix products, courant_base(): jnp.einsum('cl,lxy->cxy', rows_table, level_hot, precision=lax.Precision....  17.9 us
    mul x1, other arithmetic, on_device(): upwind_sweep(padded_cross, base_own * tables_own[1][:, None, None], 2)  17.8 us
    slice x1, local copies, waits for them, and re-layouts, on_device(): spectra[:, row_index]  14.2 us
    while x18, local copies, waits for them, and re-layouts  10.3 us
    dot_general x6, matrix products, advance(): jnp.dot(coupling, current.astype(jnp.bfloat16), preferred_element_type=jn...  8.99 us
    reshape x1, local copies, waits for them, and re-layouts, on_device(): return returned.reshape(per_group, strip_rows, columns)  7.31 us
  transfers between devices with their start and end apart: 3, of which 3 were waited for; matrix products, arithmetic and copies ran while one was open for 1% of the time, Pallas kernels for 0%

commit v1 on v0

v1 whole, which is shorter than its diff:
```python
import math

import jax
import jax.numpy as jnp
import numpy as np
from jax import lax
from jax.experimental import pallas as pl
from jax.experimental.pallas import tpu as pltpu
from jax.sharding import PartitionSpec as P

NF = 36
ND = 36
LEVELS = 8

TIME_STEP = 1.0
WIND_RATE = 0.3
BREAK_RATE = 0.8
MIXING = 0.5

LANES = 128
SUBS = 8
VMEM_LIMIT = 56 * 1024 * 1024


def edge_rows(cells, axis, width):
    count = lax.axis_size(axis)
    ends = count - 1
    head = cells[:, :width]
    tail = cells[:, -width:]
    below = lax.ppermute(tail, axis, [(i, i + 1) for i in range(ends)])
    above = lax.ppermute(head, axis, [(i + 1, i) for i in range(ends)])
    return below, above


def spectral_tables():
    frequency = np.arange(NF, dtype=np.float64)
    angle = 2.0 * math.pi / ND * (np.arange(ND) + 0.5)
    norm_total = ND * np.sum(np.power(1.1, 2.0 * frequency))
    by_frequency = np.stack([
        WIND_RATE * 1.5 * np.power(1.1, -frequency),
        np.power(1.1, 2.0 * frequency) / norm_total,
        BREAK_RATE * (frequency + 1.0) / NF,
    ])
    by_direction = np.zeros((4 * ND, SUBS))
    by_direction[:, 0] = WIND_RATE * np.tile(np.cos(angle), 4)
    by_direction[:, 1] = WIND_RATE * np.tile(np.sin(angle), 4)
    return jnp.asarray(by_frequency.astype(np.float32)), jnp.asarray(by_direction.astype(np.float32))


def take_lanes(values, index):
    return jnp.take_along_axis(values, index, axis=1, mode="promise_in_bounds")


class Layout:
    def __init__(self, rows, columns, hosts):
        self.tiles = rows // SUBS
        self.halves = columns // LANES
        self.hosts = hosts
        self.guests = [(t, h) for t in range(hosts, self.tiles) for h in range(self.halves)]
        self.blocks = [(t, h) for t in range(hosts) for h in range(self.halves)]
        self.guest_tiles = self.tiles - hosts
        self.share = hosts // self.guest_tiles if self.guest_tiles else hosts

    def guest_of(self, t, h):
        return (t // self.share) * self.halves + h

    def block_of(self, t, h):
        return t * self.halves + h


def view(ref, t, h):
    return ref[pl.ds(t * SUBS, SUBS), pl.ds(h * LANES, LANES)]


def make_plan(layout, mask, wind_u, wind_v, substeps):
    halves = layout.halves
    host_rows = layout.hosts * SUBS
    guest_rows = layout.guest_tiles * SUBS
    columns = halves * LANES

    def body(mask_ref, u_ref, v_ref, n_ref, fill_ref, spare_ref, back_ref, uo_ref, vo_ref, no_ref, spare_flag, back_flag):
        lane = lax.broadcasted_iota(jnp.int32, (SUBS, LANES), 1)

        def ranks(marked):
            total = marked
            for bit in range(7):
                step = 1 << bit
                total = total + jnp.where(lane >= step, pltpu.roll(total, step, 1), 0)
            rank = total - marked
            state = jnp.where(marked > 0, lane + LANES * (lane - rank), -1)
            for bit in range(7):
                moved = pltpu.roll(state, LANES - (1 << bit), 1)
                take = (moved >= 0) & (((moved >> (7 + bit)) & 1) == 1)
                stay = (state >= 0) & (((state >> (7 + bit)) & 1) == 0)
                state = jnp.where(take, moved, jnp.where(stay, state, -1))
            count = jnp.broadcast_to(jnp.sum(marked, axis=1, keepdims=True), (SUBS, LANES))
            return rank, jnp.maximum(state, 0) & (LANES - 1), count

        def inside(index):
            return jnp.clip(index, 0, LANES - 1)

        hole, hole_rank, hole_at, hole_count = [], [], [], []
        for t, h in layout.blocks:
            marked = 1 - view(mask_ref, t, h)
            rank, at, count = ranks(marked)
            hole.append(marked > 0)
            hole_rank.append(rank)
            hole_at.append(at)
            hole_count.append(count)
        sea, sea_rank, sea_at, sea_count = [], [], [], []
        for t, h in layout.guests:
            marked = view(mask_ref, t, h)
            rank, at, count = ranks(marked)
            sea.append(marked > 0)
            sea_rank.append(rank)
            sea_at.append(at)
            sea_count.append(count)

        guests = len(layout.guests)
        zero = jnp.zeros((SUBS, LANES), jnp.int32)
        start = []
        holes_of = [zero] * guests
        for b, (t, h) in enumerate(layout.blocks):
            j = layout.guest_of(t, h)
            start.append(holes_of[j])
            holes_of[j] = holes_of[j] + hole_count[b]
        open_of = [jnp.maximum(holes_of[j] - sea_count[j], 0) for j in range(guests)]
        left_of = [jnp.maximum(sea_count[j] - holes_of[j], 0) for j in range(guests)]
        open_start, left_start = [zero], [zero]
        for j in range(1, guests):
            open_start.append(open_start[-1] + open_of[j - 1])
            left_start.append(left_start[-1] + left_of[j - 1])

        for b, (t, h) in enumerate(layout.blocks):
            own = layout.guest_of(t, h)
            rank = start[b] + hole_rank[b]
            first = take_lanes(sea_at[own], inside(rank))
            spare = jnp.full((SUBS, LANES), -1, jnp.int32)
            extra = open_start[own] + rank - sea_count[own]
            loose = hole[b] & (rank >= sea_count[own])
            for j in range(guests):
                if j != own:
                    fits = loose & (extra >= left_start[j]) & (extra < left_start[j] + left_of[j])
                    found = take_lanes(sea_at[j], inside(extra - left_start[j] + holes_of[j]))
                    spare = jnp.where(fits, LANES * j + found, spare)
            place = (pl.ds(t * SUBS, SUBS), pl.ds(h * LANES, LANES))
            fill_ref[place] = first
            spare_ref[place] = spare
            spare_flag[b] = jnp.max(spare)
            filled = (rank < sea_count[own]) | (spare >= 0)
            for source, target in ((u_ref, uo_ref), (v_ref, vo_ref), (n_ref, no_ref)):
                value = take_lanes(view(source, *layout.guests[own]), first)
                for j, guest in enumerate(layout.guests):
                    if j != own:
                        other = take_lanes(view(source, *guest), spare & (LANES - 1))
                        value = jnp.where(spare >> 7 == j, other, value)
                if source is n_ref:
                    value = jnp.where(filled, value, 1.0)
                target[place] = jnp.where(hole[b], value, view(source, t, h))

        for j, (t, h) in enumerate(layout.guests):
            rank = sea_rank[j]
            back = jnp.full((SUBS, LANES), -1, jnp.int32)
            home = jnp.full((SUBS, LANES), 1, jnp.int32)
            extra = left_start[j] + rank - holes_of[j]
            for b, block in enumerate(layout.blocks):
                own = layout.guest_of(*block)
                if own == j:
                    at = rank
                    ok = sea[j] & (rank < holes_of[j])
                else:
                    at = extra - open_start[own] + sea_count[own]
                    ok = sea[j] & (rank >= holes_of[j])
                    ok = ok & (extra >= open_start[own]) & (extra < open_start[own] + open_of[own])
                ok = ok & (at >= start[b]) & (at < start[b] + hole_count[b])
                back = jnp.where(ok, LANES * b + take_lanes(hole_at[b], inside(at - start[b])), back)
                if own != j:
                    home = jnp.where(ok, 0, home)
            back_ref[pl.ds((t - layout.hosts) * SUBS, SUBS), pl.ds(h * LANES, LANES)] = back
            back_flag[j] = 1 - jnp.min(home)

    vmem = pl.BlockSpec(memory_space=pltpu.VMEM)
    smem = pl.BlockSpec(memory_space=pltpu.SMEM)
    whole = (host_rows, columns)
    turns = jnp.broadcast_to(substeps.astype(jnp.float32)[:, None], mask.shape)
    return pl.pallas_call(
        body,
        in_specs=[vmem] * 4,
        out_specs=[vmem] * 6 + [smem] * 2,
        out_shape=[
            jax.ShapeDtypeStruct(whole, jnp.int32),
            jax.ShapeDtypeStruct(whole, jnp.int32),
            jax.ShapeDtypeStruct((guest_rows, columns), jnp.int32),
            jax.ShapeDtypeStruct(whole, jnp.float32),
            jax.ShapeDtypeStruct(whole, jnp.float32),
            jax.ShapeDtypeStruct(whole, jnp.float32),
            jax.ShapeDtypeStruct((len(layout.blocks),), jnp.int32),
            jax.ShapeDtypeStruct((len(layout.guests),), jnp.int32),
        ],
        name="plan",
    )(mask, wind_u, wind_v, turns)


def wire_rows(layout, per_group):
    even = per_group // SUBS * SUBS
    rest = per_group - even
    return layout.hosts * even, -(-(layout.hosts * per_group) // SUBS) * SUBS, even, rest


def propagate(layout, spectrum, below, above, mask, depth_level, speed_table, group_index, plan):
    per_group, rows, columns = spectrum.shape
    groups = SUBS * layout.halves
    rest_start, pitch, even, rest = wire_rows(layout, per_group)
    steps = even // SUBS + 1
    kinds = (per_group - 2) // ND + 2
    angle = 2.0 * math.pi / ND * (np.arange(ND) + 0.5)
    turns = jnp.asarray(np.stack([np.cos(angle), np.sin(angle)]).astype(np.float32))
    packed = layout.guest_tiles > 0

    def body(*refs):
        if packed:
            (first_ref, turn_ref, speed_ref, flag_ref, spec_ref, below_ref, above_ref, mask_ref, depth_ref,
             fill_ref, spare_ref, out_ref, base_ref, sea_ref, pad_ref, field_ref) = refs
        else:
            (first_ref, turn_ref, speed_ref, spec_ref, below_ref, above_ref, mask_ref, depth_ref,
             out_ref, base_ref, sea_ref, pad_ref, field_ref) = refs
        step = pl.program_id(0)
        first = first_ref[0]
        lowest = first // ND

        @pl.when(step == 0)
        def _():
            sea_ref[...] = mask_ref[...].astype(jnp.float32)
            for k in range(kinds):
                f = jnp.minimum(lowest + k, NF - 1)
                for t in range(layout.tiles):
                    place = pl.ds(t * SUBS, SUBS)
                    level = depth_ref[place, :]
                    speed = jnp.zeros(level.shape, jnp.float32)
                    for l in range(LEVELS):
                        speed = jnp.where(level == l, speed_ref[f, l], speed)
                    base_ref[k, place, :] = speed

        lane = lax.broadcasted_iota(jnp.int32, (2 * SUBS, columns), 1)

        def sweep(centre, near, far, amount):
            one = amount * (2.0 - amount)
            two = 0.5 * amount * (amount - 1.0)
            return centre + one * (near - centre) + two * (far - centre)

        def component(cc, carry):
            c = first + step * SUBS + cc
            d = c % ND
            kind = c // ND - lowest
            cos_part = turn_ref[0, d]
            sin_part = turn_ref[1, d]
            wide_x = jnp.abs(cos_part)
            wide_y = jnp.abs(sin_part)
            pad_ref[pl.ds(SUBS - 2, 2), :] = below_ref[cc]
            pad_ref[pl.ds(rows + SUBS, 2), :] = above_ref[cc]
            pad_ref[pl.ds(SUBS, rows), :] = spec_ref[cc] * sea_ref[...]

            def run(sign_x, sign_y):
                for t in range(0, layout.tiles, 2):
                    place = pl.ds(t * SUBS, 2 * SUBS)
                    base = base_ref[kind, place, :]
                    at = (t + 1) * SUBS
                    centre = pad_ref[pl.ds(at, 2 * SUBS), :]
                    near = pad_ref[pl.ds(at - sign_x, 2 * SUBS), :]
                    far = pad_ref[pl.ds(at - 2 * sign_x, 2 * SUBS), :]
                    centre = sweep(centre, near, far, base * wide_x) * sea_ref[place, :]
                    near = pltpu.roll(centre, sign_y % columns, 1)
                    far = pltpu.roll(centre, (2 * sign_y) % columns, 1)
                    if sign_y > 0:
                        near = jnp.where(lane >= 1, near, 0.0)
                        far = jnp.where(lane >= 2, far, 0.0)
                    else:
                        near = jnp.where(lane < columns - 1, near, 0.0)
                        far = jnp.where(lane < columns - 2, far, 0.0)
                    field_ref[cc, place, :] = sweep(centre, near, far, base * wide_y)

            for sign_x in (1, -1):
                for sign_y in (1, -1):
                    right_x = cos_part >= 0.0 if sign_x > 0 else cos_part < 0.0
                    right_y = sin_part >= 0.0 if sign_y > 0 else sin_part < 0.0

                    @pl.when(right_x & right_y)
                    def _():
                        run(sign_x, sign_y)

            return carry

        lax.fori_loop(0, jnp.where(step == steps - 1, rest, SUBS), component, 0)

        def pack(count, row_of):
            for b, (t, h) in enumerate(layout.blocks):
                place = (pl.ds(t * SUBS, SUBS), pl.ds(h * LANES, LANES))

                def put(cc, value):
                    out_ref[pl.ds(h * SUBS * pitch + row_of(t, cc), SUBS, stride=pitch), :] = value

                if not packed:
                    for cc in range(count):
                        put(cc, field_ref[(cc,) + place])
                    continue
                own = layout.guests[layout.guest_of(t, h)]
                sea = sea_ref[place] > 0.0
                first = fill_ref[place]

                def base_value(cc):
                    guest = view(field_ref.at[cc], *own)
                    return jnp.where(sea, field_ref[(cc,) + place], take_lanes(guest, first))

                @pl.when(flag_ref[b] < 0)
                def _():
                    for cc in range(count):
                        put(cc, base_value(cc))

                @pl.when(flag_ref[b] >= 0)
                def _():
                    spare = spare_ref[place]
                    for cc in range(count):
                        value = base_value(cc)
                        for j, guest in enumerate(layout.guests):
                            other = take_lanes(view(field_ref.at[cc], *guest), spare & (LANES - 1))
                            value = jnp.where(spare >> 7 == j, other, value)
                        put(cc, value)

        @pl.when(step < steps - 1)
        def _():
            pack(SUBS, lambda t, cc: t * even + step * SUBS + cc)

        @pl.when(step == steps - 1)
        def _():
            pack(rest, lambda t, cc: rest_start + t * rest + cc)

    smem = pl.BlockSpec(memory_space=pltpu.SMEM)

    def fixed(array):
        return pl.BlockSpec(array.shape, lambda i: (0,) * array.ndim)

    extra_smem = [plan["spare_flag"]] if packed else []
    extra = [plan["fill"], plan["spare"]] if packed else []
    chunked = pl.BlockSpec((SUBS, rows, columns), lambda i: (i, 0, 0))
    edge = pl.BlockSpec((SUBS, 2, columns), lambda i: (i, 0, 0))
    wire = pl.pallas_call(
        body,
        grid=(steps,),
        in_specs=[smem] * (3 + len(extra_smem)) + [chunked, edge, edge, fixed(mask), fixed(depth_level)] + [fixed(a) for a in extra],
        out_specs=pl.BlockSpec((groups * pitch, LANES), lambda i: (0, 0)),
        out_shape=jax.ShapeDtypeStruct((groups * pitch, LANES), jnp.float32),
        scratch_shapes=[
            pltpu.VMEM((kinds, rows, columns), jnp.float32),
            pltpu.VMEM((rows, columns), jnp.float32),
            pltpu.VMEM((rows + 2 * SUBS, columns), jnp.float32),
            pltpu.VMEM((SUBS, rows, columns), jnp.float32),
        ],
        compiler_params=pltpu.CompilerParams(vmem_limit_bytes=VMEM_LIMIT, dimension_semantics=("arbitrary",)),
        name="propagate",
    )((group_index * per_group).reshape(1), turns, speed_table, *extra_smem, spectrum, below, above, mask, depth_level, *extra)
    return wire.reshape(groups, pitch, LANES)


def apply_source(layout, wire, per_group, east, north, turns, coupling):
    groups, pitch, _ = wire.shape
    rest_start, _, even, rest = wire_rows(layout, per_group)
    total = groups * per_group
    pairs = layout.hosts // 2
    wide = 2 * LANES
    span = 4 * ND
    most = jnp.max(turns.reshape(pairs, wide), axis=1).astype(jnp.int32)
    by_frequency, by_direction = spectral_tables()

    def body(most_ref, freq_ref, wire_ref, east_ref, north_ref, turn_ref, coupling_ref, dir_ref, out_ref,
             value_ref, round_ref, wind_ref, mix_ref):
        subrow = lax.broadcasted_iota(jnp.int32, (SUBS, wide), 0)

        def moves():
            for k in range(groups):
                yield (k * per_group, even), lambda t, k=k: (k * pitch + t * even, even)
                yield (k * per_group + even, rest), lambda t, k=k: (k * pitch + rest_start + t * rest, rest)

        def per_row(row, start, stop):
            def at(kind):
                low, high = start // ND, (stop - 1) // ND
                first = freq_ref[kind, row + low]
                if low == high:
                    return first
                return jnp.where(subrow < high * ND - start, first, freq_ref[kind, row + high])
            return at

        for pair in range(pairs):
            for half in range(2):
                lanes = pl.ds(half * LANES, LANES)
                for here, there in moves():
                    value_ref[pl.ds(*here), lanes] = wire_ref[pl.ds(*there(2 * pair + half)), :]

            def line(ref):
                row = jnp.concatenate([ref[pl.ds(2 * pair, 1), :], ref[pl.ds(2 * pair + 1, 1), :]], axis=1)
                return jnp.broadcast_to(row, (SUBS, wide))

            east_line, north_line, turn_line = line(east_ref), line(north_ref), line(turn_ref)
            step_line = TIME_STEP / turn_line
            for i in range(0, span, SUBS):
                columns = dir_ref[pl.ds(i, SUBS), :]
                wind_ref[pl.ds(i, SUBS), :] = east_line * columns[:, 0:1] + north_line * columns[:, 1:2]

            def sweep(change):
                def block(i, steep):
                    for q in range(0, span, 2 * SUBS):
                        values = []
                        for start in (q, q + SUBS):
                            at = per_row(i * 4, start, start + SUBS)
                            place = pl.ds(pl.multiple_of(i * span + start, SUBS), SUBS)
                            value = value_ref[place, :]
                            if change is not None:
                                value = change(place, start, at, value)
                                value_ref[place, :] = value
                            steep = steep + at(1) * value
                            values.append(value)
                        both = pl.ds(pl.multiple_of(i * span + q, 2 * SUBS), 2 * SUBS)
                        round_ref[both, :] = jnp.concatenate(values, axis=0).astype(jnp.bfloat16)
                    return steep

                steep = lax.fori_loop(0, total // span, block, jnp.zeros((SUBS, wide), jnp.float32))
                steepness = jnp.broadcast_to(jnp.sum(steep, axis=0, keepdims=True), (SUBS, wide))
                return steepness * steepness

            def turn(repeat, square):
                mix_ref[...] = jnp.dot(coupling_ref[...], round_ref[...], preferred_element_type=jnp.float32)
                active = repeat.astype(jnp.float32) < turn_line
                half_step = MIXING * step_line

                def change(place, start, at, value):
                    rate = jnp.maximum(0.0, wind_ref[pl.ds(start, SUBS), :] - at(0)) - at(2) * square
                    return jnp.where(active, value + (step_line * (rate * value) + half_step * mix_ref[place, :]), value)

                return sweep(change)

            lax.fori_loop(0, most_ref[pair], turn, sweep(None))
            for half in range(2):
                lanes = pl.ds(half * LANES, LANES)
                for here, there in moves():
                    out_ref[pl.ds(*there(2 * pair + half)), :] = value_ref[pl.ds(*here), lanes]

    vmem = pl.BlockSpec(memory_space=pltpu.VMEM)
    smem = pl.BlockSpec(memory_space=pltpu.SMEM)
    out = pl.pallas_call(
        body,
        in_specs=[smem] * 2 + [vmem] * 6,
        out_specs=vmem,
        out_shape=jax.ShapeDtypeStruct((groups * pitch, LANES), jnp.float32),
        scratch_shapes=[
            pltpu.VMEM((total, wide), jnp.float32),
            pltpu.VMEM((total, wide), jnp.bfloat16),
            pltpu.VMEM((span, wide), jnp.float32),
            pltpu.VMEM((total, wide), jnp.float32),
        ],
        compiler_params=pltpu.CompilerParams(vmem_limit_bytes=VMEM_LIMIT),
        name="source",
    )(most, by_frequency, wire.reshape(groups * pitch, LANES), east, north, turns, coupling, by_direction)
    return out.reshape(groups, pitch, LANES)


def unpack(layout, wire, per_group, mask, plan):
    groups, pitch, _ = wire.shape
    rest_start, _, even, rest = wire_rows(layout, per_group)
    steps = even // SUBS + 1
    rows, columns = mask.shape
    packed = layout.guest_tiles > 0

    def body(*refs):
        if packed:
            flag_ref, wire_ref, mask_ref, back_ref, out_ref = refs
        else:
            wire_ref, mask_ref, out_ref = refs
        step = pl.program_id(0)

        def spread(count, row_of):
            def get(t, h, cc):
                return wire_ref[pl.ds(h * SUBS * pitch + row_of(t, cc), SUBS, stride=pitch), :]

            for t, h in layout.blocks:
                place = (pl.ds(t * SUBS, SUBS), pl.ds(h * LANES, LANES))
                sea = mask_ref[place] > 0
                for cc in range(count):
                    out_ref[(cc,) + place] = jnp.where(sea, get(t, h, cc), 0.0)
            for j, (t, h) in enumerate(layout.guests):
                place = (pl.ds(t * SUBS, SUBS), pl.ds(h * LANES, LANES))
                back = back_ref[pl.ds((t - layout.hosts) * SUBS, SUBS), pl.ds(h * LANES, LANES)]
                index = back & (LANES - 1)
                block = back >> 7

                def fetch(blocks):
                    for cc in range(count):
                        value = jnp.zeros((SUBS, LANES), jnp.float32)
                        for b in blocks:
                            found = take_lanes(get(*layout.blocks[b], cc), index)
                            value = jnp.where(block == b, found, value)
                        out_ref[(cc,) + place] = value

                near = [b for b, at in enumerate(layout.blocks) if layout.guest_of(*at) == j]

                @pl.when(flag_ref[j] == 0)
                def _():
                    fetch(near)

                @pl.when(flag_ref[j] != 0)
                def _():
                    fetch(range(len(layout.blocks)))

        @pl.when(step < steps - 1)
        def _():
            spread(SUBS, lambda t, cc: t * even + step * SUBS + cc)

        @pl.when(step == steps - 1)
        def _():
            spread(rest, lambda t, cc: rest_start + t * rest + cc)

    smem = pl.BlockSpec(memory_space=pltpu.SMEM)
    fixed = pl.BlockSpec((groups * pitch, LANES), lambda i: (0, 0))
    fixed_mask = pl.BlockSpec((rows, columns), lambda i: (0, 0))
    extra_smem = [plan["back_flag"]] if packed else []
    extra = [plan["back"]] if packed else []
    return pl.pallas_call(
        body,
        grid=(steps,),
        in_specs=[smem] * len(extra_smem) + [fixed, fixed_mask] + [pl.BlockSpec(a.shape, lambda i: (0, 0)) for a in extra],
        out_specs=pl.BlockSpec((SUBS, rows, columns), lambda i: (i, 0, 0)),
        out_shape=jax.ShapeDtypeStruct((per_group, rows, columns), jnp.float32),
        compiler_params=pltpu.CompilerParams(vmem_limit_bytes=VMEM_LIMIT, dimension_semantics=("arbitrary",)),
        name="unpack",
    )(*extra_smem, wire.reshape(groups * pitch, LANES), mask, *extra)


def regroup(wire):
    return lax.all_to_all(wire, "comp", split_axis=0, concat_axis=0, tiled=True)


def on_device(spectrum, mask, depth_level, speed_table, wind_u, wind_v, substeps, coupling):
    per_group, rows, columns = spectrum.shape
    group_index = lax.axis_index("comp")
    tiles = rows // SUBS
    edges = jnp.concatenate([spectrum[:, :2], spectrum[:, -2:]], axis=1) * jnp.concatenate([mask[:2], mask[-2:]], axis=0).astype(jnp.float32)[None]
    below, above = edge_rows(edges, "space", 2)
    subrow = group_index % SUBS
    half = group_index // SUBS

    def own(array, hosts):
        parts = array.reshape(hosts, SUBS, columns // LANES, LANES)
        return lax.dynamic_slice(parts, (0, subrow, half, 0), (hosts, 1, 1, LANES)).reshape(hosts, LANES)

    def step(hosts):
        layout = Layout(rows, columns, hosts)
        if hosts < tiles:
            fill, spare, back, east, north, turns, spare_flag, back_flag = make_plan(layout, mask, wind_u, wind_v, substeps)
            plan = dict(fill=fill, spare=spare, back=back, spare_flag=spare_flag, back_flag=back_flag)
        else:
            plan = {}
            east, north = wind_u, wind_v
            turns = jnp.broadcast_to(substeps.astype(jnp.float32)[:, None], mask.shape)
        wire = propagate(layout, spectrum, below, above, mask, depth_level, speed_table, group_index, plan)
        wire = regroup(wire)
        wire = apply_source(layout, wire, per_group, own(east, hosts), own(north, hosts), own(turns, hosts), coupling)
        wire = regroup(wire)
        return unpack(layout, wire, per_group, mask, plan)

    hosts = tiles * 3 // 4
    busy = jnp.sum(mask.reshape(tiles, SUBS, columns), axis=(0, 2))
    return lax.cond(jnp.all(busy <= hosts * columns), lambda: step(hosts), lambda: step(tiles))


def solution(mesh):
    placed = (
        P("comp", "space", None),
        P("space", None),
        P("space", None),
        P(),
        P("space", None),
        P("space", None),
        P("space"),
        P(),
    )
    return jax.shard_map(
        on_device, mesh=mesh, in_specs=placed, out_specs=P("comp", "space", None), check_vma=False
    )
```

time: 316 us -> 217 us (0.69)
  Pallas kernels: 0 us -> 72.4 us
  blocking collectives: 103 us -> 54.1 us
  local copies, waits for them, and re-layouts: 53.9 us -> 9.44 us
  other arithmetic: 31.9 us -> 4.01 us
  matrix products: 27.1 us -> 0 us
  waiting for transfers between devices: 77.3 us -> 59.2 us
  loops' own time: 6.47 us -> 0.26 us
    pallas_call x0 -> x4, Pallas kernels: none -> 72.4 us  [the longest x1 29.1 us: propagate(): pl.pallas_call(body, grid=(steps,), in_specs=[smem] * (3 + len(extra_smem...]
    all_to_all x1, blocking collectives: 103 us -> 54.1 us  [regroup(): return lax.all_to_all(wire, 'comp', split_axis=0, concat_axis=0, tiled=True)]
    dot_general x8 -> x0, matrix products: 27.1 us -> none  [the longest x1 17.9 us: courant_base(): jnp.einsum('cl,lxy->cxy', rows_table, level_hot, precision=lax.Precision....]
    mul x9 -> x1, other arithmetic: 23.5 us -> 0.16 us  [on_device(): jnp.concatenate([spectrum[:, :2], spectrum[:, -2:]], axis=1)]
    all_to_all x1, waiting for transfers between devices: 73.1 us -> 58.8 us  [regroup(): return lax.all_to_all(wire, 'comp', split_axis=0, concat_axis=0, tiled=True)]
    reshape x2 -> x0, local copies, waits for them, and re-layouts: 14.4 us -> none  [the longest x1 7.31 us: on_device(): return returned.reshape(per_group, strip_rows, columns)]
    slice x4 -> x3, local copies, waits for them, and re-layouts: 15.8 us -> 2.26 us  [the longest x1 1.41 us: on_device(): spectrum[:, :2]]
    while x18 -> x0, local copies, waits for them, and re-layouts: 10.3 us -> none
  transfers between devices with their start and end apart: 3 -> 3, of which waited for: 3 -> 2; matrix products, arithmetic and copies ran while one was open for 1% -> 3% of each run, Pallas kernels for 0% -> 0%
where the time goes in v1:
time: 217 us; the launch traced here: 213 us
  Pallas kernels  72.4 us (33%)
  waiting for transfers between devices  59.2 us (27%)
  blocking collectives  54.1 us (25%)
  starting transfers between devices  12.8 us (6%)
  local copies, waits for them, and re-layouts  9.44 us (4%)
  other arithmetic  4.01 us (2%)
    all_to_all x1, waiting for transfers between devices, regroup(): return lax.all_to_all(wire, 'comp', split_axis=0, concat_axis=0, tiled=True)  58.8 us
    all_to_all x1, blocking collectives, regroup(): return lax.all_to_all(wire, 'comp', split_axis=0, concat_axis=0, tiled=True)  54.1 us
    pallas_call x1, Pallas kernels, propagate(): pl.pallas_call(body, grid=(steps,), in_specs=[smem] * (3 + len(extra_smem...  29.1 us
    pallas_call x1, Pallas kernels, apply_source(): pl.pallas_call(body, in_specs=[smem] * 2 + [vmem] * 6, out_specs=vmem, ou...  27.4 us
    pallas_call x1, Pallas kernels, unpack(): pl.pallas_call(body, grid=(steps,), in_specs=[smem] * len(extra_smem) + [...  8.91 us
    all_to_all x1, starting transfers between devices, regroup(): return lax.all_to_all(wire, 'comp', split_axis=0, concat_axis=0, tiled=True)  7.23 us
    pallas_call x1, Pallas kernels, make_plan(): pl.pallas_call(body, in_specs=[vmem] * 4, out_specs=[vmem] * 6 + [smem] *...  7.04 us
  transfers between devices with their start and end apart: 3, of which 2 were waited for; matrix products, arithmetic and copies ran while one was open for 3% of the time, Pallas kernels for 0%

profile of v1, /device:TPU:32, one launch (start us, length us, event | category | flops | bytes accessed | tf_op | source)
XLA Modules:
  0.0 213.0 jit_solution(11075216887816130999)
XLA Ops:
  0.0 1.4 fusion.1
  1.4 0.7 fusion.3
  2.1 0.2 maximum_multiply_fusion
  2.3 0.1 fusion.2
  2.4 1.9 collective-permute-start
  4.4 3.6 %collective-permute-start.1 = (f32[81,2,256]{2,1,0:T(2,128)S(1)}, f32[81,2,256]{2,1,0:T(2,128)S(1)}, u32[]{:S(2)}, u32[]{:S(2)}) collective-permute-start(f32[81,2,256]{2,1,0:T(2,128)S(1)} %get-tuple-element.217), channel_id=1, source_target_pairs={{1,0},{2,1},{3,2},{4,3},{5,4},{6,5},{7,6},{9,8},{10,9},{11,10},{12... | collective-permute-start | bytes 497672 | tf_op jit(solution)/shard_map/ppermute | solution.py:31
  8.0 0.9 reduce_sum.10
  9.0 0.1 reduce_sum.14
  9.1 0.6 compare_reduce_fusion
  10.4 0.0 collective-permute-done
  10.4 0.4 collective-permute-done.1
  10.9 199.7 %conditional.1 = (f32[81,64,256]{2,1,0:T(8,128)S(1)}) conditional(s32[]{:T(128)} %convert_element_type.22, (s32[64]{0:T(128)}, s32[]{:T(128)}, s32[]{:T(128)}, f32[2,36]{1,0:T(2,128)}, f32[36,8]{0,1:T(8,128)}, /*index=5*/f32[81,64,256]{2,1,0:T(8,128)}, f32[81,2,256]{2,1,0:T(2,128)S(1)}, f32[81,2,256]{2,1,0:T(2,128)S(1)}, s32[64,256]{1,0:T(8,128)}, ...), branch_computations={%region_3.0_spmd, %region_6.9_spmd} | conditional | flops 1095 | bytes 26849768 | solution.py:570
  10.9 0.7 convert_element_type.18
  11.5 1.4 copy.37.refs_2_
  12.9 0.7 broadcast_in_dim.9.n_ref
  13.6 7.0 %plan.1 = (s32[48,256]{1,0:T(8,128)}, s32[48,256]{1,0:T(8,128)}, s32[16,256]{1,0:T(8,128)}, f32[48,256]{1,0:T(8,128)}, f32[48,256]{1,0:T(8,128)}, /*index=5*/f32[48,256]{1,0:T(8,128)}, s32[12]{0:T(128)}, s32[4]{0:T(128)}) custom-call(s32[64,256]{1,0:T(8,128)} %get-tuple-element.88.mask_ref.refs_7_.refs_2_, f32[64,256]{1,0:T(8,128)} %get-tuple-element.89.u_ref, ...), custom_call_target="tpu_custom_call" | custom-call | tf_op jit(solution)/shard_map/cond/branch_1_fun/plan/pallas_call | solution.py:186
  20.6 29.1 %propagate.3 = f32[7808,128]{1,0:T(8,128)} custom-call(s32[1]{0:T(128)} %bitcast.10.refs_0_, f32[2,36]{1,0:T(2,128)} %get-tuple-element.98.refs_1_, f32[36,8]{1,0:T(8,128)} %copy.37.refs_2_, s32[12]{0:T(128)} %get-tuple-element.100.refs_3_, f32[81,64,256]{2,1,0:T(8,128)} %get-tuple-element.101.refs_4_, f32[81,2,256]{2,1,0:T(2,128)S(1)} %get-tuple-element.102.refs_5_, ...), custom_call_target="tpu_custom_call" | custom-call | tf_op jit(solution)/shard_map/cond/branch_1_fun/propagate/pallas_call | solution.py:346
  49.7 0.0 copy-start.4
  49.7 0.0 copy-start.6
  49.8 7.2 %all-to-all-start.2 = ((f32[16,488,128]{2,1,0:T(8,128)}), f32[16,488,128]{2,1,0:T(8,128)}, u32[]{:S(2)}, u32[]{:S(2)}) async-start(f32[16,488,128]{2,1,0:T(8,128)} %bitcast.33), calls=%async_computation.2 | async-start | bytes 7995392 | tf_op jit(solution)/shard_map/cond/branch_1_fun/all_to_all | solution.py:537
  57.0 0.9 fusion
  57.9 0.1 reduce_max.24
  58.0 0.1 reduce_max.25
  58.1 0.6 convert_element_type.19.most_ref
  58.7 0.8 constant_dynamic-slice_fusion
  59.4 0.6 copy.48
  60.0 0.6 copy.47
  60.6 0.6 copy.49
  61.2 58.8 %all-to-all-done.2 = f32[16,488,128]{2,1,0:T(8,128)} async-done(((f32[16,488,128]{2,1,0:T(8,128)}), f32[16,488,128]{2,1,0:T(8,128)}, u32[]{:S(2)}, u32[]{:S(2)}) %all-to-all-start.2) | async-done | bytes 3997728 | tf_op jit(solution)/shard_map/cond/branch_1_fun/all_to_all | solution.py:537
  120.0 0.0 copy-done.4
  120.0 0.0 copy-done.6
  120.0 27.4 %source.3 = f32[7808,128]{1,0:T(8,128)} custom-call(s32[3]{0:T(128)} %convert_element_type.19.most_ref, f32[3,36]{1,0:T(4,128)S(1)} %copy-done.6, f32[7808,128]{1,0:T(8,128)} %bitcast.12.wire_ref, f32[6,128]{1,0:T(8,128)} %bitcast.38, f32[6,128]{1,0:T(8,128)} %bitcast.39, f32[6,128]{1,0:T(8,128)} %bitcast.40, ...), custom_call_target="tpu_custom_call" | custom-call | tf_op jit(solution)/shard_map/cond/branch_1_fun/source/pallas_call | solution.py:448
  147.3 0.0 copy-start.2
  147.3 54.1 %all_to_all.17 = f32[16,488,128]{2,1,0:T(8,128)} all-to-all(f32[16,488,128]{2,1,0:T(8,128)} %bitcast.34), channel_id=1, replica_groups=mesh['comp'=16,'space'=8] {'comp'}, dimensions={0} | all-to-all | bytes 7995392 | tf_op jit(solution)/shard_map/cond/branch_1_fun/all_to_all | solution.py:537
  201.4 0.0 copy-done.2
  201.4 8.9 %unpack.3 = f32[81,64,256]{2,1,0:T(8,128)S(1)} custom-call(s32[4]{0:T(128)} %get-tuple-element.92.refs_0_, f32[7808,128]{1,0:T(8,128)} %bitcast.35, s32[64,256]{1,0:T(8,128)S(1)} %copy-done.2, s32[16,256]{1,0:T(8,128)} %get-tuple-element.111.refs_3_), custom_call_target="tpu_custom_call" | custom-call | tf_op jit(solution)/shard_map/cond/branch_1_fun/unpack/pallas_call | solution.py:525
  210.6 0.0 copy-start
  210.6 2.4 %copy-done = f32[81,64,256]{2,1,0:T(8,128)} copy-done((f32[81,64,256]{2,1,0:T(8,128)}, f32[81,64,256]{2,1,0:T(8,128)S(1)}, u32[]{:S(2)}) %copy-start) | copy-done | bytes 5308440
  (2 shorter events, 0.0 us)
Async XLA Ops:
  2.4 8.0 %collective-permute-start = (f32[81,2,256]{2,1,0:T(2,128)S(1)}, f32[81,2,256]{2,1,0:T(2,128)S(1)}, u32[]{:S(2)}, u32[]{:S(2)}) collective-permute-start(f32[81,2,256]{2,1,0:T(2,128)S(1)} %get-tuple-element.218), channel_id=1, source_target_pairs={{0,1},{1,2},{2,3},{3,4},{4,5},{5,6},{6,7},{8,9},{9,10},{10,11},{11... | collective-permute-start | bytes 497672 | tf_op jit(solution)/shard_map/ppermute | solution.py:30
  4.4 6.5 %collective-permute-start.1 = (f32[81,2,256]{2,1,0:T(2,128)S(1)}, f32[81,2,256]{2,1,0:T(2,128)S(1)}, u32[]{:S(2)}, u32[]{:S(2)}) collective-permute-start(f32[81,2,256]{2,1,0:T(2,128)S(1)} %get-tuple-element.217), channel_id=1, source_target_pairs={{1,0},{2,1},{3,2},{4,3},{5,4},{6,5},{7,6},{9,8},{10,9},{11,10},{12... | collective-permute-start | bytes 497672 | tf_op jit(solution)/shard_map/ppermute | solution.py:31
  49.7 70.2 %copy-start.4 = (f32[144,8]{1,0:T(8,128)S(1)}, f32[144,8]{1,0:T(8,128)}, u32[]{:S(2)}) copy-start(f32[144,8]{1,0:T(8,128)} %get-tuple-element.110.dir_ref) | copy-start | bytes 13828 | tf_op jit(solution)/shard_map/cond
  49.7 70.2 %copy-start.6 = (f32[3,36]{1,0:T(4,128)S(1)}, f32[3,36]{1,0:T(4,128)}, u32[]{:S(2)}) copy-start(f32[3,36]{1,0:T(4,128)} %get-tuple-element.96.freq_ref) | copy-start | bytes 1300 | tf_op jit(solution)/shard_map/cond
  49.8 70.2 %all-to-all-start.2 = ((f32[16,488,128]{2,1,0:T(8,128)}), f32[16,488,128]{2,1,0:T(8,128)}, u32[]{:S(2)}, u32[]{:S(2)}) async-start(f32[16,488,128]{2,1,0:T(8,128)} %bitcast.33), calls=%async_computation.2 | async-start | bytes 7995392 | tf_op jit(solution)/shard_map/cond/branch_1_fun/all_to_all | solution.py:537
  147.3 54.1 %copy-start.2 = (s32[64,256]{1,0:T(8,128)S(1)}, s32[64,256]{1,0:T(8,128)}, u32[]{:S(2)}) copy-start(s32[64,256]{1,0:T(8,128)} %get-tuple-element.88.mask_ref.refs_7_.refs_2_) | copy-start | bytes 196612 | tf_op jit(solution)/shard_map/cond
  210.6 2.4 %copy-start = (f32[81,64,256]{2,1,0:T(8,128)}, f32[81,64,256]{2,1,0:T(8,128)S(1)}, u32[]{:S(2)}) copy-start(f32[81,64,256]{2,1,0:T(8,128)S(1)} %get-tuple-element.227) | copy-start | bytes 15925252

commit v2 on v0

v2 whole, which is shorter than its diff:
```python
import math

import jax
import jax.numpy as jnp
import numpy as np
from jax import lax
from jax.experimental import pallas as pl
from jax.experimental.pallas import tpu as pltpu
from jax.sharding import PartitionSpec as P

NF = 36
ND = 36
LEVELS = 8

TIME_STEP = 1.0
WIND_RATE = 0.3
BREAK_RATE = 0.8
MIXING = 0.5

LANES = 128
SUBS = 8
VMEM_LIMIT = 56 * 1024 * 1024


def edge_rows(cells, axis, width):
    count = lax.axis_size(axis)
    ends = count - 1
    head = cells[:, :width]
    tail = cells[:, -width:]
    below = lax.ppermute(tail, axis, [(i, i + 1) for i in range(ends)])
    above = lax.ppermute(head, axis, [(i + 1, i) for i in range(ends)])
    return below, above


def spectral_tables(period):
    frequency = np.arange(NF, dtype=np.float64)
    angle = 2.0 * math.pi / ND * (np.arange(ND) + 0.5)
    norm_total = ND * np.sum(np.power(1.1, 2.0 * frequency))
    phase = WIND_RATE * 1.5 * np.power(1.1, -frequency)
    weight = np.power(1.1, 2.0 * frequency) / norm_total
    damping = BREAK_RATE * (frequency + 1.0) / NF
    by_direction = np.zeros((period, SUBS))
    by_direction[:, 0] = WIND_RATE * np.tile(np.cos(angle), period // ND)
    by_direction[:, 1] = WIND_RATE * np.tile(np.sin(angle), period // ND)
    return phase, weight, damping, jnp.asarray(by_direction.astype(np.float32))


def take_lanes(values, index):
    return jnp.take_along_axis(values, index, axis=1, mode="promise_in_bounds")


class Layout:
    def __init__(self, rows, columns, hosts, guests):
        self.tiles = rows // SUBS
        self.halves = columns // LANES
        self.hosts = hosts
        self.guest_tiles = guests
        self.guests = [(t, h) for t in guests for h in range(self.halves)]
        self.blocks = [(i, h) for i in range(len(hosts)) for h in range(self.halves)]
        self.share = len(hosts) // len(guests) if guests else 0

    def guest_of(self, i, h):
        return (i // self.share) * self.halves + h


def view(ref, t, h):
    return ref[pl.ds(t * SUBS, SUBS), pl.ds(h * LANES, LANES)]


def count_blocks(layout, mask_ref):
    marked = [1 - view(mask_ref, layout.hosts[i], h) for i, h in layout.blocks]
    marked = jnp.concatenate(marked + [view(mask_ref, t, h) for t, h in layout.guests], axis=0)
    lane = lax.broadcasted_iota(jnp.int32, marked.shape, 1)
    upto = (lax.broadcasted_iota(jnp.int32, (LANES, LANES), 0) <= lax.broadcasted_iota(jnp.int32, (LANES, LANES), 1)).astype(jnp.bfloat16)
    total = jnp.dot(marked.astype(jnp.bfloat16), upto, preferred_element_type=jnp.float32).astype(jnp.int32)
    rank = total - marked
    state = jnp.where(marked > 0, lane + LANES * (lane - rank), -1)
    for bit in range(7):
        moved = pltpu.roll(state, LANES - (1 << bit), 1)
        take = (moved >= 0) & (((moved >> (7 + bit)) & 1) == 1)
        stay = (state >= 0) & (((state >> (7 + bit)) & 1) == 0)
        state = jnp.where(take, moved, jnp.where(stay, state, -1))
    place = jnp.maximum(state, 0) & (LANES - 1)
    count = jnp.broadcast_to(total[:, LANES - 1:], marked.shape)

    def parts(array):
        each = [array[i:i + SUBS] for i in range(0, array.shape[0], SUBS)]
        return each[:len(layout.blocks)], each[len(layout.blocks):]

    return parts(marked), parts(rank), parts(place), parts(count)


class Plan:
    def __init__(self, layout, mask_ref):
        (hole, self.sea), (self.hole_rank, self.sea_rank), (self.hole_at, self.sea_at), counts = count_blocks(layout, mask_ref)
        self.hole_count, self.sea_count = counts
        self.hole = [m > 0 for m in hole]
        self.sea = [m > 0 for m in self.sea]
        guests = len(layout.guests)
        zero = jnp.zeros((SUBS, LANES), jnp.int32)
        self.start = []
        self.holes_of = [zero] * guests
        for b, at in enumerate(layout.blocks):
            j = layout.guest_of(*at)
            self.start.append(self.holes_of[j])
            self.holes_of[j] = self.holes_of[j] + self.hole_count[b]
        self.open_of = [jnp.maximum(self.holes_of[j] - self.sea_count[j], 0) for j in range(guests)]
        self.left_of = [jnp.maximum(self.sea_count[j] - self.holes_of[j], 0) for j in range(guests)]
        self.open_start, self.left_start = [zero], [zero]
        for j in range(1, guests):
            self.open_start.append(self.open_start[-1] + self.open_of[j - 1])
            self.left_start.append(self.left_start[-1] + self.left_of[j - 1])


def inside(index):
    return jnp.clip(index, 0, LANES - 1)


VMEM_SPEC = pl.BlockSpec(memory_space=pltpu.VMEM)
SMEM_SPEC = pl.BlockSpec(memory_space=pltpu.SMEM)


def make_plan(layout, mask, wind_u, wind_v, substeps):
    columns = mask.shape[1]

    def body(mask_ref, u_ref, v_ref, n_ref, fill_ref, spare_ref, back_ref, uo_ref, vo_ref, no_ref, flag_ref, back_flag, fits_ref):
        p = Plan(layout, mask_ref)
        subrow = lax.broadcasted_iota(jnp.int32, (SUBS, LANES), 0)
        ranks = []

        def turns_of(t):
            result = jnp.zeros((SUBS, LANES), jnp.int32)
            for r in range(SUBS):
                result = jnp.where(subrow == r, n_ref[t * SUBS + r], result)
            return result.astype(jnp.float32)

        every = {t: turns_of(t) for t in range(layout.tiles)}
        for b, (i, h) in enumerate(layout.blocks):
            own = layout.guest_of(i, h)
            rank = p.start[b] + p.hole_rank[b]
            ranks.append(rank)
            first = take_lanes(p.sea_at[own], inside(rank))
            place = (pl.ds(i * SUBS, SUBS), pl.ds(h * LANES, LANES))
            fill_ref[place] = first
            flag_ref[b] = -1
            hole = p.hole[b]
            for source, target in ((u_ref, uo_ref), (v_ref, vo_ref)):
                value = take_lanes(view(source, *layout.guests[own]), first)
                target[place] = jnp.where(hole, value, view(source, layout.hosts[i], h))
            guest = jnp.where(rank < p.sea_count[own], every[layout.guests[own][0]], 1.0)
            no_ref[place] = jnp.where(hole, guest, every[layout.hosts[i]])

        for j, (t, h) in enumerate(layout.guests):
            rank = p.sea_rank[j]
            back = jnp.full((SUBS, LANES), -1, jnp.int32)
            for b, block in enumerate(layout.blocks):
                if layout.guest_of(*block) == j:
                    ok = p.sea[j] & (rank >= p.start[b]) & (rank < p.start[b] + p.hole_count[b])
                    back = jnp.where(ok, LANES * b + take_lanes(p.hole_at[b], inside(rank - p.start[b])), back)
            back_ref[pl.ds(layout.guest_tiles.index(t) * SUBS, SUBS), pl.ds(h * LANES, LANES)] = back
            back_flag[j] = 0

        left = sum(p.left_of)
        flag_ref[len(layout.blocks)] = jnp.max(left)
        fits_ref[0] = (jnp.max(left - sum(p.open_of)) <= 0).astype(jnp.int32)

        @pl.when(jnp.max(left) > 0)
        def _():
            for b, (i, h) in enumerate(layout.blocks):
                own = layout.guest_of(i, h)
                spare = jnp.full((SUBS, LANES), -1, jnp.int32)
                extra = p.open_start[own] + ranks[b] - p.sea_count[own]
                loose = p.hole[b] & (ranks[b] >= p.sea_count[own])
                for j in range(len(layout.guests)):
                    if j != own:
                        ok = loose & (extra >= p.left_start[j]) & (extra < p.left_start[j] + p.left_of[j])
                        found = take_lanes(p.sea_at[j], inside(extra - p.left_start[j] + p.holes_of[j]))
                        spare = jnp.where(ok, LANES * j + found, spare)
                place = (pl.ds(i * SUBS, SUBS), pl.ds(h * LANES, LANES))
                spare_ref[place] = spare
                most = jnp.max(spare)
                flag_ref[b] = most

                @pl.when(most >= 0)
                def _():
                    for j, guest in enumerate(layout.guests):
                        chosen = spare >> 7 == j
                        for source, target in ((u_ref, uo_ref), (v_ref, vo_ref)):
                            other = take_lanes(view(source, *guest), spare & (LANES - 1))
                            target[place] = jnp.where(chosen, other, target[place])
                        no_ref[place] = jnp.where(chosen, every[guest[0]], no_ref[place])

            for j, (t, h) in enumerate(layout.guests):
                @pl.when(jnp.max(p.left_of[j]) > 0)
                def _():
                    place = (pl.ds(layout.guest_tiles.index(t) * SUBS, SUBS), pl.ds(h * LANES, LANES))
                    back = back_ref[place]
                    rank = p.sea_rank[j]
                    extra = p.left_start[j] + rank - p.holes_of[j]
                    for b, block in enumerate(layout.blocks):
                        own = layout.guest_of(*block)
                        if own != j:
                            at = extra - p.open_start[own] + p.sea_count[own]
                            ok = p.sea[j] & (rank >= p.holes_of[j])
                            ok = ok & (extra >= p.open_start[own]) & (extra < p.open_start[own] + p.open_of[own])
                            ok = ok & (at >= p.start[b]) & (at < p.start[b] + p.hole_count[b])
                            back = jnp.where(ok, LANES * b + take_lanes(p.hole_at[b], inside(at - p.start[b])), back)
                    back_ref[place] = back
                    back_flag[j] = 1

    whole = (len(layout.hosts) * SUBS, columns)
    return pl.pallas_call(
        body,
        in_specs=[VMEM_SPEC] * 3 + [SMEM_SPEC],
        out_specs=[VMEM_SPEC] * 6 + [SMEM_SPEC] * 3,
        out_shape=[
            jax.ShapeDtypeStruct(whole, jnp.int32),
            jax.ShapeDtypeStruct(whole, jnp.int32),
            jax.ShapeDtypeStruct((len(layout.guest_tiles) * SUBS, columns), jnp.int32),
            jax.ShapeDtypeStruct(whole, jnp.float32),
            jax.ShapeDtypeStruct(whole, jnp.float32),
            jax.ShapeDtypeStruct(whole, jnp.float32),
            jax.ShapeDtypeStruct((len(layout.blocks) + 1,), jnp.int32),
            jax.ShapeDtypeStruct((len(layout.guests),), jnp.int32),
            jax.ShapeDtypeStruct((1,), jnp.int32),
        ],
        name="plan",
    )(mask, wind_u, wind_v, substeps)


class Wire:
    def __init__(self, layout, per_group, tiles):
        self.tiles = tiles
        self.even = per_group // SUBS * SUBS
        self.rest = per_group - self.even
        self.rest_start = len(tiles) * self.even
        self.pitch = -(-(len(tiles) * per_group) // SUBS) * SUBS
        self.groups = SUBS * layout.halves
        self.blocks = [b for b, (i, h) in enumerate(layout.blocks) if i in tiles]

    def row(self, t, c):
        t = t - self.tiles[0]
        return jnp.where(c < self.even, t * self.even + c, self.rest_start + t * self.rest + c - self.even)

    def lines(self, t, h, c):
        return pl.ds(h * SUBS * self.pitch + self.row(t, c), SUBS, stride=self.pitch)


def propagate(layout, wire, spectrum, edges, mask, depth_level, speed_table, group_index, filling):
    per_group, rows, columns = spectrum.shape
    run = ND // 4
    steps = per_group // run
    angle = 2.0 * math.pi / ND * (np.arange(ND) + 0.5)
    turns = jnp.asarray(np.abs(np.stack([np.cos(angle), np.sin(angle)])).astype(np.float32))
    packed = len(layout.guests) > 0
    tiles = sorted([layout.hosts[i] for i in wire.tiles] + layout.guest_tiles)
    edged = len(edges) > 0

    def body(*refs):
        refs = list(refs)
        first_ref, turn_ref, speed_ref = refs[:3]
        flag_ref = refs[3] if packed else None
        refs = refs[3 + packed:]
        spec_ref = refs[0]
        below_ref, above_ref = refs[1:3] if edged else (None, None)
        refs = refs[1 + 2 * edged:]
        mask_ref, depth_ref = refs[:2]
        fill_ref, spare_ref = refs[2:4] if packed else (None, None)
        out_ref, base_ref, sea_ref, pad_ref, field_ref = refs[2 + 2 * packed:]
        step = pl.program_id(0)
        start = first_ref[0] + step * run
        f = start // ND

        @pl.when(step == 0)
        def _():
            sea_ref[...] = mask_ref[...].astype(jnp.float32)

        @pl.when((step == 0) | (start % ND == 0))
        def _():
            for t in tiles:
                place = pl.ds(t * SUBS, SUBS)
                level = depth_ref[place, :]
                speed = jnp.zeros(level.shape, jnp.float32)
                for l in range(LEVELS):
                    speed = jnp.where(level == l, speed_ref[l, f], speed)
                base_ref[place, :] = speed

        lane = lax.broadcasted_iota(jnp.int32, (SUBS, LANES), 1)

        def sweep(centre, near, far, amount):
            one = amount * (2.0 - amount)
            two = 0.5 * amount * (amount - 1.0)
            return centre + one * (near - centre) + two * (far - centre)

        def shifted(parts, by):
            turned = [pltpu.roll(part, by % LANES, 1) for part in parts]
            edge = jnp.zeros_like(turned[0])
            if by > 0:
                return [jnp.where(lane >= by, turned[i], turned[i - 1] if i else edge) for i in range(len(parts))]
            ends = turned[1:] + [edge]
            return [jnp.where(lane < LANES + by, turned[i], ends[i]) for i in range(len(parts))]

        def run_all(sign_x, sign_y):
            def component(cc, carry):
                d = start % ND + cc
                wide_x = turn_ref[0, d]
                wide_y = turn_ref[1, d]
                needed = sorted({n for t in tiles for n in (t, t - sign_x) if 0 <= n < layout.tiles})
                if edged:
                    pad_ref[cc, pl.ds(SUBS - 2, 2), :] = below_ref[step * run + cc]
                    pad_ref[cc, pl.ds(rows + SUBS, 2), :] = above_ref[step * run + cc]
                for t in needed:
                    place = pl.ds(t * SUBS, SUBS)
                    pad_ref[cc, pl.ds((t + 1) * SUBS, SUBS), :] = spec_ref[cc, place, :] * sea_ref[place, :]
                for t in tiles:
                    place = pl.ds(t * SUBS, SUBS)
                    at = (t + 1) * SUBS
                    base = base_ref[place, :]
                    centre = pad_ref[cc, pl.ds(at, SUBS), :]
                    near = pad_ref[cc, pl.ds(at - sign_x, SUBS), :]
                    far = pad_ref[cc, pl.ds(at - 2 * sign_x, SUBS), :]
                    centre = sweep(centre, near, far, base * wide_x) * sea_ref[place, :]
                    amount = base * wide_y
                    parts = [centre[:, h * LANES:(h + 1) * LANES] for h in range(layout.halves)]
                    near = shifted(parts, sign_y)
                    far = shifted(parts, 2 * sign_y)
                    for h in range(layout.halves):
                        lanes = slice(h * LANES, (h + 1) * LANES)
                        field_ref[cc, place, lanes] = sweep(parts[h], near[h], far[h], amount[:, lanes])
                return carry

            lax.fori_loop(0, run, component, 0, unroll=9)

        quadrant = (start % ND) // run
        for at, signs in enumerate(((1, 1), (-1, 1), (-1, -1), (1, -1))):
            pl.when(quadrant == at)(lambda signs=signs: run_all(*signs))

        def put(t, h, cc, value):
            out_ref[wire.lines(t, h, step * run + cc), :] = value

        def base_value(t, h, cc):
            value = view(field_ref.at[cc], layout.hosts[t], h)
            if packed:
                guest = view(field_ref.at[cc], *layout.guests[layout.guest_of(t, h)])
                value = jnp.where(view(sea_ref, layout.hosts[t], h) > 0.0, value, take_lanes(guest, view(fill_ref, t, h)))
            return value

        for b in wire.blocks:
            for cc in range(run):
                put(*layout.blocks[b], cc, base_value(*layout.blocks[b], cc))
        if not packed:
            return

        def fill_spare(b):
            t, h = layout.blocks[b]
            spare = view(spare_ref, t, h)
            for cc in range(run):
                value = base_value(t, h, cc)
                for j, guest in enumerate(layout.guests):
                    if j != layout.guest_of(t, h):
                        other = take_lanes(view(field_ref.at[cc], *guest), spare & (LANES - 1))
                        value = jnp.where(spare >> 7 == j, other, value)
                put(t, h, cc, value)

        @pl.when(flag_ref[len(layout.blocks)] > 0)
        def _():
            for b in wire.blocks:
                pl.when(flag_ref[b] >= 0)(lambda b=b: fill_spare(b))

    smem = pl.BlockSpec(memory_space=pltpu.SMEM)

    def fixed(array):
        return pl.BlockSpec(array.shape, lambda i: (0,) * array.ndim)

    extra_smem = [filling[2]] if packed else []
    extra = list(filling[:2]) if packed else []
    shape = (wire.groups * wire.pitch, LANES)
    out = pl.pallas_call(
        body,
        grid=(steps,),
        in_specs=[smem] * (3 + len(extra_smem)) + [pl.BlockSpec((run, rows, columns), lambda i: (i, 0, 0))] + [fixed(edge) for edge in edges] + [fixed(mask), fixed(depth_level)] + [fixed(a) for a in extra],
        out_specs=pl.BlockSpec(shape, lambda i: (0, 0)),
        out_shape=jax.ShapeDtypeStruct(shape, jnp.float32),
        scratch_shapes=[
            pltpu.VMEM((rows, columns), jnp.float32),
            pltpu.VMEM((rows, columns), jnp.float32),
            pltpu.VMEM((run, rows + 2 * SUBS, columns), jnp.float32),
            pltpu.VMEM((run, rows, columns), jnp.float32),
        ],
        compiler_params=pltpu.CompilerParams(vmem_limit_bytes=VMEM_LIMIT, dimension_semantics=("arbitrary",)),
        name="propagate",
    )((group_index * per_group).reshape(1), turns, speed_table.T, *extra_smem, spectrum, *edges, mask, depth_level, *extra)
    return out.reshape(wire.groups, wire.pitch, LANES)


def apply_source(wire, values, per_group, spot, east, north, turns, coupling):
    groups, pitch, even = wire.groups, wire.pitch, wire.even
    total = groups * per_group
    pairs = len(wire.tiles) // 2
    period = 2 * ND
    pieces = 9
    piece = total // pieces
    phase, weight, damping, by_direction = spectral_tables(period)

    def body(spot_ref, main_ref, last_ref, east_ref, north_ref, turn_ref, coupling_ref, dir_ref, out_ref,
             low_ref, high_ref, round_ref, wind_ref, mix_ref, stage_ref, rest_ref, sem):
        pair = pl.program_id(0)
        value_refs = (low_ref, high_ref)
        subrow = lax.broadcasted_iota(jnp.int32, (SUBS, LANES), 0)

        def constant(table, start):
            low, high = start // ND, (start + SUBS - 1) // ND
            if low == high:
                return float(table[low])
            return jnp.where(subrow < high * ND - start, float(table[low]), float(table[high]))

        def line(ref, half):
            tile = ref[pl.ds(pl.multiple_of((2 * pair + half) * SUBS, SUBS), SUBS), :]
            tile = jnp.where(spot_ref[1] == 0, tile[:, :LANES], tile[:, LANES:])
            row = jnp.sum(jnp.where(subrow == spot_ref[0], tile, 0.0), axis=0, keepdims=True)
            return jnp.broadcast_to(row, (SUBS, LANES))

        @pl.when(pair == 0)
        def _():
            for k in range(groups):
                rest_ref[pl.ds(k * SUBS, SUBS), :] = last_ref[k]

        turn_line = [line(turn_ref, half) for half in range(2)]
        step_line = [TIME_STEP / t for t in turn_line]
        for half, ref in enumerate(value_refs):
            for k in range(groups):
                ref[pl.ds(k * per_group, even), :] = main_ref[k, pl.ds(half * even, even), :]
            ref[pl.ds(even, groups, stride=per_group), :] = rest_ref[pl.ds(2 * pair + half, groups, stride=SUBS), :]
            east_line, north_line = line(east_ref, half), line(north_ref, half)
            for i in range(0, period, SUBS):
                columns = dir_ref[pl.ds(i, SUBS), :]
                wind_ref[pl.ds(i, SUBS), pl.ds(half * LANES, LANES)] = east_line * columns[:, 0:1] + north_line * columns[:, 1:2]

        def sweep(change):
            squares = []
            for half, ref in enumerate(value_refs):
                steep = jnp.zeros((SUBS, LANES), jnp.float32)
                for f in range(0, NF, 2):
                    sums = [None, None]
                    for start in range(f * ND, (f + 2) * ND, SUBS):
                        place = pl.ds(start, SUBS)
                        value = ref[place, :]
                        if change is not None:
                            value = change(half, start, value)
                            ref[place, :] = value
                        low, high = start // ND, (start + SUBS - 1) // ND
                        if low != high:
                            steep = steep + constant(weight, start) * value
                        else:
                            sums[low - f] = value if sums[low - f] is None else sums[low - f] + value
                    steep = steep + float(weight[f]) * sums[0] + float(weight[f + 1]) * sums[1]
                steepness = jnp.broadcast_to(jnp.sum(steep, axis=0, keepdims=True), (SUBS, LANES))
                squares.append(steepness * steepness)
            return tuple(squares)

        def round_all():
            for half, ref in enumerate(value_refs):
                for start in range(0, total, 2 * SUBS):
                    place = pl.ds(start, 2 * SUBS)
                    round_ref[place, pl.ds(half * LANES, LANES)] = ref[place, :].astype(jnp.bfloat16)

        def turn(repeat, squares):
            for i in range(pieces):
                place = pl.ds(i * piece, piece)
                mix_ref[place, :] = jnp.dot(coupling_ref[place, :], round_ref[...], preferred_element_type=jnp.float32)

            def change(half, start, value):
                lanes = pl.ds(half * LANES, LANES)
                rate = jnp.maximum(0.0, wind_ref[pl.ds(start % period, SUBS), lanes] - constant(phase, start))
                rate = rate - constant(damping, start) * squares[half]
                step = step_line[half]
                moved = value + step * (rate * value + MIXING * mix_ref[pl.ds(start, SUBS), lanes])
                return jnp.where(repeat.astype(jnp.float32) < turn_line[half], moved, value)

            squares = sweep(change)
            round_all()
            return squares

        squares = sweep(None)
        round_all()
        most = jnp.max(jnp.maximum(turn_line[0], turn_line[1])).astype(jnp.int32)
        lax.fori_loop(0, most, turn, squares)

        for half, ref in enumerate(value_refs):
            for k in range(groups):
                stage_ref[pair, k, pl.ds(half * even, even), :] = ref[pl.ds(k * per_group, even), :]
            rest_ref[pl.ds(2 * pair + half, groups, stride=SUBS), :] = ref[pl.ds(even, groups, stride=per_group), :]

        def send(p):
            return pltpu.make_async_copy(stage_ref.at[p], out_ref.at[:, pl.ds(p * 2 * even, 2 * even), :], sem.at[p])

        send(pair).start()

        @pl.when(pair == pairs - 1)
        def _():
            final = [
                pltpu.make_async_copy(rest_ref.at[pl.ds(k * SUBS, SUBS)], out_ref.at[k, pl.ds(pitch - SUBS, SUBS), :], sem.at[pairs + k])
                for k in range(groups)
            ]
            for copy in final:
                copy.start()
            for copy in final:
                copy.wait()
            for p in range(pairs):
                send(p).wait()

    def fixed(array):
        return pl.BlockSpec(array.shape, lambda i: (0,) * array.ndim)

    return pl.pallas_call(
        body,
        grid=(pairs,),
        in_specs=[
            SMEM_SPEC,
            pl.BlockSpec((groups, 2 * even, LANES), lambda i: (0, i, 0)),
            pl.BlockSpec((groups, SUBS, LANES), lambda i: (0, pitch // SUBS - 1, 0)),
        ]
        + [fixed(array) for array in (east, north, turns, coupling, by_direction)],
        out_specs=pl.BlockSpec(memory_space=pl.ANY),
        out_shape=jax.ShapeDtypeStruct((groups, pitch, LANES), jnp.float32),
        scratch_shapes=[
            pltpu.VMEM((total, LANES), jnp.float32),
            pltpu.VMEM((total, LANES), jnp.float32),
            pltpu.VMEM((total, 2 * LANES), jnp.bfloat16),
            pltpu.VMEM((period, 2 * LANES), jnp.float32),
            pltpu.VMEM((total, 2 * LANES), jnp.float32),
            pltpu.VMEM((pairs, groups, 2 * even, LANES), jnp.float32),
            pltpu.VMEM((groups * SUBS, LANES), jnp.float32),
            pltpu.SemaphoreType.DMA((pairs + groups,)),
        ],
        compiler_params=pltpu.CompilerParams(vmem_limit_bytes=VMEM_LIMIT, dimension_semantics=("arbitrary",)),
        name="source",
    )(spot, values, values, east, north, turns, coupling, by_direction)


def unpack(layout, wires, arrays, per_group, mask, back):
    run = ND // 4
    steps = per_group // run
    rows, columns = mask.shape
    packed = len(layout.guests) > 0

    def body(*refs):
        refs = list(refs)
        flag_ref = refs.pop(0) if packed else None
        wire_refs = [refs.pop(0) for _ in wires]
        mask_ref = refs.pop(0)
        back_ref = refs.pop(0) if packed else None
        target_ref, held_ref, sem = refs
        step = pl.program_id(0)
        out_ref = held_ref.at[pl.ds(step * run, run)]

        def get(t, h, cc):
            for wire, ref in zip(wires, wire_refs):
                if t in wire.tiles:
                    return ref[wire.lines(t, h, step * run + cc), :]

        def fetch(j, blocks):
            t, h = layout.guests[j]
            place = (pl.ds(t * SUBS, SUBS), pl.ds(h * LANES, LANES))
            back = view(back_ref, layout.guest_tiles.index(t), h)
            for cc in range(run):
                value = jnp.zeros((SUBS, LANES), jnp.float32)
                for b in blocks:
                    found = take_lanes(get(*layout.blocks[b], cc), back & (LANES - 1))
                    value = jnp.where(back >> 7 == b, found, value)
                out_ref[(cc,) + place] = value

        for i, h in layout.blocks:
            place = (pl.ds(layout.hosts[i] * SUBS, SUBS), pl.ds(h * LANES, LANES))
            sea = mask_ref[place] > 0
            for cc in range(run):
                out_ref[(cc,) + place] = jnp.where(sea, get(i, h, cc), 0.0)
        for j in range(len(layout.guests)):
            fetch(j, [b for b, at in enumerate(layout.blocks) if layout.guest_of(*at) == j])
        for j in range(len(layout.guests)):
            pl.when(flag_ref[j] != 0)(lambda j=j: fetch(j, range(len(layout.blocks))))

        def send(at):
            place = pl.ds(at * run, run)
            return pltpu.make_async_copy(held_ref.at[place], target_ref.at[place], sem.at[at])

        send(step).start()

        @pl.when(step == steps - 1)
        def _():
            for at in range(steps):
                send(at).wait()

    smem = pl.BlockSpec(memory_space=pltpu.SMEM)
    extra_smem = [back[1]] if packed else []
    inputs = [array.reshape(-1, LANES) for array in arrays] + [mask] + ([back[0]] if packed else [])
    return pl.pallas_call(
        body,
        grid=(steps,),
        in_specs=[smem] * len(extra_smem) + [pl.BlockSpec(a.shape, lambda i: (0, 0)) for a in inputs],
        out_specs=pl.BlockSpec(memory_space=pltpu.HBM),
        out_shape=pltpu.HBM((per_group, rows, columns), jnp.float32),
        scratch_shapes=[pltpu.VMEM((per_group, rows, columns), jnp.float32), pltpu.SemaphoreType.DMA((steps,))],
        compiler_params=pltpu.CompilerParams(vmem_limit_bytes=VMEM_LIMIT, dimension_semantics=("arbitrary",)),
        name="unpack",
    )(*extra_smem, *inputs)


def regroup(wire):
    return lax.all_to_all(wire, "comp", split_axis=0, concat_axis=0, tiled=True)


def on_device(spectrum, mask, depth_level, speed_table, wind_u, wind_v, substeps, coupling):
    per_group, rows, columns = spectrum.shape
    group_index = lax.axis_index("comp")
    tiles = rows // SUBS
    edges = jnp.concatenate([spectrum[:, :2], spectrum[:, -2:]], axis=1) * jnp.concatenate([mask[:2], mask[-2:]], axis=0).astype(jnp.float32)[None]
    edges = edge_rows(edges, "space", 2)
    spot = jnp.stack([group_index % SUBS, group_index // SUBS])
    guests = [tiles // 2 - 1, tiles // 2]
    hosts = [t for t in range(tiles) if t not in guests]

    def step(hosts, guests, filling, east, north, turns, back):
        layout = Layout(rows, columns, hosts, guests)
        wire = Wire(layout, per_group, range(len(hosts)))
        values = regroup(propagate(layout, wire, spectrum, edges, mask, depth_level, speed_table, group_index, filling))
        values = regroup(apply_source(wire, values, per_group, spot, east, north, turns, coupling))
        return unpack(layout, [wire], [values], per_group, mask, back)

    fill, spare, back, east, north, turns, flag, back_flag, fits = make_plan(
        Layout(rows, columns, hosts, guests), mask, wind_u, wind_v, substeps
    )
    every = jnp.broadcast_to(substeps.astype(jnp.float32)[:, None], mask.shape)
    return lax.cond(
        fits[0] > 0,
        lambda: step(hosts, guests, (fill, spare, flag), east, north, turns, (back, back_flag)),
        lambda: step(list(range(tiles)), [], None, wind_u, wind_v, every, None),
    )


def solution(mesh):
    placed = (
        P("comp", "space", None),
        P("space", None),
        P("space", None),
        P(),
        P("space", None),
        P("space", None),
        P("space"),
        P(),
    )
    return jax.shard_map(
        on_device, mesh=mesh, in_specs=placed, out_specs=P("comp", "space", None), check_vma=False
    )
```

time: 316 us -> 159 us (0.50)
  the two profiles are of different devices: /device:TPU:32 before, /device:TPU:64 now
where the time goes in v2:
time: 159 us
  blocking collectives  110 us (69%)
  Pallas kernels  38.8 us (24%)
  starting transfers between devices  5.56 us (3%)
  local copies, waits for them, and re-layouts  2.27 us (1%)
    all_to_all x2, blocking collectives, regroup(): return lax.all_to_all(wire, 'comp', split_axis=0, concat_axis=0, tiled=True)  110 us
    pallas_call x1, Pallas kernels, apply_source(): pl.pallas_call(body, grid=(pairs,), in_specs=[SMEM_SPEC, pl.BlockSpec((gr...  15.8 us
    pallas_call x1, Pallas kernels, propagate(): pl.pallas_call(body, grid=(steps,), in_specs=[smem] * (3 + len(extra_smem...  15 us
    pallas_call x1, Pallas kernels, unpack(): pl.pallas_call(body, grid=(steps,), in_specs=[smem] * len(extra_smem) + [...  5.58 us
    ppermute x1, starting transfers between devices, edge_rows(): above = lax.ppermute(head, axis, [(i + 1, i) for i in range(ends)])  3.64 us
  transfers between devices with their start and end apart: 2, of which 0 were waited for; matrix products, arithmetic and copies ran while one was open for 0% of the time, Pallas kernels for 2%

profile of v2, /device:TPU:64, one launch (start us, length us, event | category | flops | bytes accessed | tf_op | source)
XLA Modules:
  0.0 159.0 jit_solution(2640684263709153017)
XLA Ops:
  0.0 0.7 fusion.2
  0.7 1.4 fusion
  2.1 0.2 maximum_multiply_fusion
  2.3 0.1 fusion.1
  2.4 1.9 %collective-permute-start = (f32[81,2,256]{2,1,0:T(2,128)S(1)}, f32[81,2,256]{2,1,0:T(2,128)S(1)}, u32[]{:S(2)}, u32[]{:S(2)}) collective-permute-start(f32[81,2,256]{2,1,0:T(2,128)S(1)} %get-tuple-element.130), channel_id=1, source_target_pairs={{0,1},{1,2},{2,3},{3,4},{4,5},{5,6},{6,7},{8,9},{9,10},{10,11},{11... | collective-permute-start | bytes 497672 | tf_op jit(solution)/shard_map/ppermute | solution.py:30
  4.4 3.6 %collective-permute-start.1 = (f32[81,2,256]{2,1,0:T(2,128)S(1)}, f32[81,2,256]{2,1,0:T(2,128)S(1)}, u32[]{:S(2)}, u32[]{:S(2)}) collective-permute-start(f32[81,2,256]{2,1,0:T(2,128)S(1)} %get-tuple-element.129), channel_id=1, source_target_pairs={{1,0},{2,1},{3,2},{4,3},{5,4},{6,5},{7,6},{9,8},{10,9},{11,10},{12... | collective-permute-start | bytes 497672 | tf_op jit(solution)/shard_map/ppermute | solution.py:31
  8.0 0.7 convert_element_type.19
  8.7 2.4 %plan.1 = (s32[48,256]{1,0:T(8,128)S(1)}, s32[48,256]{1,0:T(8,128)S(1)}, s32[16,256]{1,0:T(8,128)S(1)}, f32[48,256]{1,0:T(8,128)S(1)}, f32[48,256]{1,0:T(8,128)S...) custom-call(s32[64,256]{1,0:T(8,128)} %mask_ref.1, f32[64,256]{1,0:T(8,128)} %u_ref.1, ...), custom_call_target="tpu_custom_call" | custom-call | tf_op jit(solution)/shard_map/plan/pallas_call | solution.py:212
  11.8 0.1 pad_add_fusion
  11.8 0.0 collective-permute-done
  11.8 0.0 collective-permute-done.1
  11.9 147.0 %conditional.1 = (f32[81,64,256]{2,1,0:T(8,128)}) conditional(s32[]{:T(128)} %bitcast.8, (s32[]{:T(128)}, f32[36,8]{0,1:T(8,128)}, f32[2,36]{1,0:T(2,128)}, f32[81,64,256]{2,1,0:T(8,128)}, f32[81,2,256]{2,1,0:T(2,128)S(1)}, /*index=5*/f32[81,2,256]{2,1,0:T(2,128)S(1)}, s32[64,256]{1,0:T(8,128)}, s32[64,256]{1,0:T(8,128)}, f32[64]{0:T(128)S(1)}, ...), branch_computations={%region_0.1_spmd, %region_1.2_spmd} | conditional | flops 1 | bytes 35532192 | solution.py:634
  12.0 15.0 %propagate.3 = f32[7808,128]{1,0:T(8,128)} custom-call(s32[1]{0:T(128)} %bitcast.4.refs_0_, f32[2,36]{1,0:T(2,128)} %get-tuple-element.92.refs_1_, f32[8,36]{1,0:T(8,128)} %bitcast.16, s32[13]{0:T(128)S(1)} %get-tuple-element.94.refs_3_, f32[81,64,256]{2,1,0:T(8,128)} %get-tuple-element.95.refs_4_, f32[81,2,256]{2,1,0:T(2,128)S(1)} %get-tuple-element.96.refs_5_, ...), custom_call_target="tpu_custom_call" | custom-call | tf_op jit(solution)/shard_map/cond/branch_1_fun/propagate/pallas_call | solution.py:378
  27.1 0.0 copy-start.1
  27.1 0.0 copy-start.7
  27.1 57.4 %all_to_all.18.main_ref.last_ref = f32[16,488,128]{2,1,0:T(8,128)} all-to-all(f32[16,488,128]{2,1,0:T(8,128)} %bitcast.13), channel_id=1, replica_groups=mesh['comp'=16,'space'=8] {'comp'}, dimensions={0} | all-to-all | bytes 7995392 | tf_op jit(solution)/shard_map/cond/branch_1_fun/all_to_all | solution.py:610
  84.4 0.0 copy-done.1
  84.4 0.0 copy-done.7
  84.4 15.8 %source.3 = f32[16,488,128]{2,1,0:T(8,128)} custom-call(s32[2]{0:T(128)S(1)} %get-tuple-element.90.spot_ref, f32[16,488,128]{2,1,0:T(8,128)} %all_to_all.18.main_ref.last_ref, f32[16,488,128]{2,1,0:T(8,128)} %all_to_all.18.main_ref.last_ref, f32[48,256]{1,0:T(8,128)S(1)} %get-tuple-element.102.east_ref, f32[48,256]{1,0:T(8,128)S(1)} %get-tuple-element.103.north_ref, ...), custom_call_target="tpu_custom_call" | custom-call | tf_op jit(solution)/shard_map/cond/branch_1_fun/source/pallas_call | solution.py:515
  100.2 0.0 copy-start.3
  100.2 52.8 %all_to_all.19 = f32[16,488,128]{2,1,0:T(8,128)} all-to-all(f32[16,488,128]{2,1,0:T(8,128)} %source.3), channel_id=1, replica_groups=mesh['comp'=16,'space'=8] {'comp'}, dimensions={0} | all-to-all | bytes 7995392 | tf_op jit(solution)/shard_map/cond/branch_1_fun/all_to_all | solution.py:610
  153.0 0.0 copy-done.3
  153.0 5.6 %unpack.3 = f32[81,64,256]{2,1,0:T(8,128)} custom-call(s32[4]{0:T(128)S(1)} %get-tuple-element.89.refs_0_, f32[7808,128]{1,0:T(8,128)} %bitcast.14, s32[64,256]{1,0:T(8,128)S(1)} %copy-done.3, s32[16,256]{1,0:T(8,128)S(1)} %get-tuple-element.107.refs_3_), custom_call_target="tpu_custom_call" | custom-call | tf_op jit(solution)/shard_map/cond/branch_1_fun/unpack/pallas_call | solution.py:597
  (1 shorter events, 0.0 us)
Async XLA Ops:
  2.4 9.4 %collective-permute-start = (f32[81,2,256]{2,1,0:T(2,128)S(1)}, f32[81,2,256]{2,1,0:T(2,128)S(1)}, u32[]{:S(2)}, u32[]{:S(2)}) collective-permute-start(f32[81,2,256]{2,1,0:T(2,128)S(1)} %get-tuple-element.130), channel_id=1, source_target_pairs={{0,1},{1,2},{2,3},{3,4},{4,5},{5,6},{6,7},{8,9},{9,10},{10,11},{11... | collective-permute-start | bytes 497672 | tf_op jit(solution)/shard_map/ppermute | solution.py:30
  4.4 7.5 %collective-permute-start.1 = (f32[81,2,256]{2,1,0:T(2,128)S(1)}, f32[81,2,256]{2,1,0:T(2,128)S(1)}, u32[]{:S(2)}, u32[]{:S(2)}) collective-permute-start(f32[81,2,256]{2,1,0:T(2,128)S(1)} %get-tuple-element.129), channel_id=1, source_target_pairs={{1,0},{2,1},{3,2},{4,3},{5,4},{6,5},{7,6},{9,8},{10,9},{11,10},{12... | collective-permute-start | bytes 497672 | tf_op jit(solution)/shard_map/ppermute | solution.py:31
  27.1 57.4 %copy-start.1 = (bf16[1296,1296]{1,0:T(8,128)(2,1)S(1)}, bf16[1296,1296]{1,0:T(8,128)(2,1)}, u32[]{:S(2)}) copy-start(bf16[1296,1296]{1,0:T(8,128)(2,1)} %get-tuple-element.105.coupling_ref) | copy-start | bytes 10077700 | tf_op jit(solution)/shard_map/cond
  27.1 57.4 %copy-start.7 = (f32[72,8]{1,0:T(8,128)S(1)}, f32[72,8]{1,0:T(8,128)}, u32[]{:S(2)}) copy-start(f32[72,8]{1,0:T(8,128)} %get-tuple-element.106.dir_ref) | copy-start | bytes 6916 | tf_op jit(solution)/shard_map/cond
  100.2 52.8 %copy-start.3 = (s32[64,256]{1,0:T(8,128)S(1)}, s32[64,256]{1,0:T(8,128)}, u32[]{:S(2)}) copy-start(s32[64,256]{1,0:T(8,128)} %get-tuple-element.98.refs_7_.refs_2_) | copy-start | bytes 196612 | tf_op jit(solution)/shard_map/cond

commit v3 on v2

--- a/solution.py
+++ b/solution.py
@@ -19,7 +19,7 @@
 
 LANES = 128
 SUBS = 8
-VMEM_LIMIT = 56 * 1024 * 1024
+MIB = 1024 * 1024
 
 
 def edge_rows(cells, axis, width):
@@ -166,29 +166,24 @@
 
         @pl.when(jnp.max(left) > 0)
         def _():
+            spare_ref[...] = jnp.full(spare_ref.shape, -1, jnp.int32)
+            for j, guest in enumerate(layout.guests):
+                @pl.when(jnp.max(p.left_of[j]) > 0)
+                def _():
+                    for b, (i, h) in enumerate(layout.blocks):
+                        own = layout.guest_of(i, h)
+                        if own == j:
+                            continue
+                        extra = p.open_start[own] + ranks[b] - p.sea_count[own] - p.left_start[j]
+                        ok = p.hole[b] & (ranks[b] >= p.sea_count[own]) & (extra >= 0) & (extra < p.left_of[j])
+                        found = take_lanes(p.sea_at[j], inside(extra + p.holes_of[j]))
+                        place = (pl.ds(i * SUBS, SUBS), pl.ds(h * LANES, LANES))
+                        spare_ref[place] = jnp.where(ok, LANES * j + found, spare_ref[place])
+                        for source, target in ((u_ref, uo_ref), (v_ref, vo_ref)):
+                            target[place] = jnp.where(ok, take_lanes(view(source, *guest), found), target[place])
+                        no_ref[place] = jnp.where(ok, every[guest[0]], no_ref[place])
             for b, (i, h) in enumerate(layout.blocks):
-                own = layout.guest_of(i, h)
-                spare = jnp.full((SUBS, LANES), -1, jnp.int32)
-                extra = p.open_start[own] + ranks[b] - p.sea_count[own]
-                loose = p.hole[b] & (ranks[b] >= p.sea_count[own])
-                for j in range(len(layout.guests)):
-                    if j != own:
-                        ok = loose & (extra >= p.left_start[j]) & (extra < p.left_start[j] + p.left_of[j])
-                        found = take_lanes(p.sea_at[j], inside(extra - p.left_start[j] + p.holes_of[j]))
-                        spare = jnp.where(ok, LANES * j + found, spare)
-                place = (pl.ds(i * SUBS, SUBS), pl.ds(h * LANES, LANES))
-                spare_ref[place] = spare
-                most = jnp.max(spare)
-                flag_ref[b] = most
-
-                @pl.when(most >= 0)
-                def _():
-                    for j, guest in enumerate(layout.guests):
-                        chosen = spare >> 7 == j
-                        for source, target in ((u_ref, uo_ref), (v_ref, vo_ref)):
-                            other = take_lanes(view(source, *guest), spare & (LANES - 1))
-                            target[place] = jnp.where(chosen, other, target[place])
-                        no_ref[place] = jnp.where(chosen, every[guest[0]], no_ref[place])
+                flag_ref[b] = jnp.max(view(spare_ref, i, h))
 
             for j, (t, h) in enumerate(layout.guests):
                 @pl.when(jnp.max(p.left_of[j]) > 0)
@@ -289,7 +284,7 @@
 
         def sweep(centre, near, far, amount):
             one = amount * (2.0 - amount)
-            two = 0.5 * amount * (amount - 1.0)
+            two = 0.5 * (amount - one)
             return centre + one * (near - centre) + two * (far - centre)
 
         def shifted(parts, by):
@@ -379,7 +374,7 @@
         body,
         grid=(steps,),
         in_specs=[smem] * (3 + len(extra_smem)) + [pl.BlockSpec((run, rows, columns), lambda i: (i, 0, 0))] + [fixed(edge) for edge in edges] + [fixed(mask), fixed(depth_level)] + [fixed(a) for a in extra],
-        out_specs=pl.BlockSpec(shape, lambda i: (0, 0)),
+        out_specs=VMEM_SPEC,
         out_shape=jax.ShapeDtypeStruct(shape, jnp.float32),
         scratch_shapes=[
             pltpu.VMEM((rows, columns), jnp.float32),
@@ -387,7 +382,7 @@
             pltpu.VMEM((run, rows + 2 * SUBS, columns), jnp.float32),
             pltpu.VMEM((run, rows, columns), jnp.float32),
         ],
-        compiler_params=pltpu.CompilerParams(vmem_limit_bytes=VMEM_LIMIT, dimension_semantics=("arbitrary",)),
+        compiler_params=pltpu.CompilerParams(vmem_limit_bytes=24 * MIB, dimension_semantics=("arbitrary",)),
         name="propagate",
     )((group_index * per_group).reshape(1), turns, speed_table.T, *extra_smem, spectrum, *edges, mask, depth_level, *extra)
     return out.reshape(wire.groups, wire.pitch, LANES)
@@ -402,8 +397,8 @@
     piece = total // pieces
     phase, weight, damping, by_direction = spectral_tables(period)
 
-    def body(spot_ref, main_ref, last_ref, east_ref, north_ref, turn_ref, coupling_ref, dir_ref, out_ref,
-             low_ref, high_ref, round_ref, wind_ref, mix_ref, stage_ref, rest_ref, sem):
+    def body(spot_ref, wire_ref, east_ref, north_ref, turn_ref, coupling_ref, dir_ref, out_ref,
+             low_ref, high_ref, round_ref, wind_ref, mix_ref, rest_ref):
         pair = pl.program_id(0)
         value_refs = (low_ref, high_ref)
         subrow = lax.broadcasted_iota(jnp.int32, (SUBS, LANES), 0)
@@ -423,13 +418,16 @@
         @pl.when(pair == 0)
         def _():
             for k in range(groups):
-                rest_ref[pl.ds(k * SUBS, SUBS), :] = last_ref[k]
+                rest_ref[pl.ds(k * SUBS, SUBS), :] = wire_ref[k, pl.ds(pitch - SUBS, SUBS), :]
+
+        def rows_of(half):
+            return pl.ds(pl.multiple_of((2 * pair + half) * even, SUBS), even)
 
         turn_line = [line(turn_ref, half) for half in range(2)]
         step_line = [TIME_STEP / t for t in turn_line]
         for half, ref in enumerate(value_refs):
             for k in range(groups):
-                ref[pl.ds(k * per_group, even), :] = main_ref[k, pl.ds(half * even, even), :]
+                ref[pl.ds(k * per_group, even), :] = wire_ref[k, rows_of(half), :]
             ref[pl.ds(even, groups, stride=per_group), :] = rest_ref[pl.ds(2 * pair + half, groups, stride=SUBS), :]
             east_line, north_line = line(east_ref, half), line(north_ref, half)
             for i in range(0, period, SUBS):
@@ -488,40 +486,19 @@
 
         for half, ref in enumerate(value_refs):
             for k in range(groups):
-                stage_ref[pair, k, pl.ds(half * even, even), :] = ref[pl.ds(k * per_group, even), :]
+                out_ref[k, rows_of(half), :] = ref[pl.ds(k * per_group, even), :]
             rest_ref[pl.ds(2 * pair + half, groups, stride=SUBS), :] = ref[pl.ds(even, groups, stride=per_group), :]
-
-        def send(p):
-            return pltpu.make_async_copy(stage_ref.at[p], out_ref.at[:, pl.ds(p * 2 * even, 2 * even), :], sem.at[p])
-
-        send(pair).start()
 
         @pl.when(pair == pairs - 1)
         def _():
-            final = [
-                pltpu.make_async_copy(rest_ref.at[pl.ds(k * SUBS, SUBS)], out_ref.at[k, pl.ds(pitch - SUBS, SUBS), :], sem.at[pairs + k])
-                for k in range(groups)
-            ]
-            for copy in final:
-                copy.start()
-            for copy in final:
-                copy.wait()
-            for p in range(pairs):
-                send(p).wait()
-
-    def fixed(array):
-        return pl.BlockSpec(array.shape, lambda i: (0,) * array.ndim)
+            for k in range(groups):
+                out_ref[k, pl.ds(pitch - SUBS, SUBS), :] = rest_ref[pl.ds(k * SUBS, SUBS), :]
 
     return pl.pallas_call(
         body,
         grid=(pairs,),
-        in_specs=[
-            SMEM_SPEC,
-            pl.BlockSpec((groups, 2 * even, LANES), lambda i: (0, i, 0)),
-            pl.BlockSpec((groups, SUBS, LANES), lambda i: (0, pitch // SUBS - 1, 0)),
-        ]
-        + [fixed(array) for array in (east, north, turns, coupling, by_direction)],
-        out_specs=pl.BlockSpec(memory_space=pl.ANY),
+        in_specs=[SMEM_SPEC] + [VMEM_SPEC] * 6,
+        out_specs=VMEM_SPEC,
         out_shape=jax.ShapeDtypeStruct((groups, pitch, LANES), jnp.float32),
         scratch_shapes=[
             pltpu.VMEM((total, LANES), jnp.float32),
@@ -529,13 +506,11 @@
             pltpu.VMEM((total, 2 * LANES), jnp.bfloat16),
             pltpu.VMEM((period, 2 * LANES), jnp.float32),
             pltpu.VMEM((total, 2 * LANES), jnp.float32),
-            pltpu.VMEM((pairs, groups, 2 * even, LANES), jnp.float32),
             pltpu.VMEM((groups * SUBS, LANES), jnp.float32),
-            pltpu.SemaphoreType.DMA((pairs + groups,)),
         ],
-        compiler_params=pltpu.CompilerParams(vmem_limit_bytes=VMEM_LIMIT, dimension_semantics=("arbitrary",)),
+        compiler_params=pltpu.CompilerParams(vmem_limit_bytes=32 * MIB, dimension_semantics=("arbitrary",)),
         name="source",
-    )(spot, values, values, east, north, turns, coupling, by_direction)
+    )(spot, values, east, north, turns, coupling, by_direction)
 
 
 def unpack(layout, wires, arrays, per_group, mask, back):
@@ -597,11 +572,11 @@
     return pl.pallas_call(
         body,
         grid=(steps,),
-        in_specs=[smem] * len(extra_smem) + [pl.BlockSpec(a.shape, lambda i: (0, 0)) for a in inputs],
+        in_specs=[smem] * len(extra_smem) + [VMEM_SPEC] * len(inputs),
         out_specs=pl.BlockSpec(memory_space=pltpu.HBM),
         out_shape=pltpu.HBM((per_group, rows, columns), jnp.float32),
         scratch_shapes=[pltpu.VMEM((per_group, rows, columns), jnp.float32), pltpu.SemaphoreType.DMA((steps,))],
-        compiler_params=pltpu.CompilerParams(vmem_limit_bytes=VMEM_LIMIT, dimension_semantics=("arbitrary",)),
+        compiler_params=pltpu.CompilerParams(vmem_limit_bytes=24 * MIB, dimension_semantics=("arbitrary",)),
         name="unpack",
     )(*extra_smem, *inputs)
 

time: 159 us -> 155 us (0.975)
  the two profiles are of different devices: /device:TPU:64 before, /device:TPU:32 now
where the time goes in v3:
time: 155 us; the launch traced here: 154 us
  blocking collectives  114 us (74%)
  Pallas kernels  30.1 us (19%)
  starting transfers between devices  5.56 us (4%)
  local copies, waits for them, and re-layouts  2.28 us (1%)
    all_to_all x2, blocking collectives, regroup(): return lax.all_to_all(wire, 'comp', split_axis=0, concat_axis=0, tiled=True)  114 us
    pallas_call x1, Pallas kernels, propagate(): pl.pallas_call(body, grid=(steps,), in_specs=[smem] * (3 + len(extra_smem...  12.7 us
    pallas_call x1, Pallas kernels, apply_source(): pl.pallas_call(body, grid=(pairs,), in_specs=[SMEM_SPEC] + [VMEM_SPEC] *...  11 us
    pallas_call x1, Pallas kernels, unpack(): pl.pallas_call(body, grid=(steps,), in_specs=[smem] * len(extra_smem) + [...  3.93 us
    ppermute x1, starting transfers between devices, edge_rows(): above = lax.ppermute(head, axis, [(i + 1, i) for i in range(ends)])  3.64 us
  transfers between devices with their start and end apart: 2, of which 0 were waited for; matrix products, arithmetic and copies ran while one was open for 0% of the time, Pallas kernels for 2%

profile of v3, /device:TPU:32, one launch (start us, length us, event | category | flops | bytes accessed | tf_op | source)
XLA Modules:
  0.0 153.8 jit_solution(9028236615333118885)
XLA Ops:
  0.0 0.7 fusion.2
  0.7 1.4 fusion
  2.1 0.2 maximum_multiply_fusion
  2.3 0.1 fusion.1
  2.4 1.9 %collective-permute-start = (f32[81,2,256]{2,1,0:T(2,128)S(1)}, f32[81,2,256]{2,1,0:T(2,128)S(1)}, u32[]{:S(2)}, u32[]{:S(2)}) collective-permute-start(f32[81,2,256]{2,1,0:T(2,128)S(1)} %get-tuple-element.130), channel_id=1, source_target_pairs={{0,1},{1,2},{2,3},{3,4},{4,5},{5,6},{6,7},{8,9},{9,10},{10,11},{11... | collective-permute-start | bytes 497672 | tf_op jit(solution)/shard_map/ppermute | solution.py:30
  4.4 3.6 %collective-permute-start.1 = (f32[81,2,256]{2,1,0:T(2,128)S(1)}, f32[81,2,256]{2,1,0:T(2,128)S(1)}, u32[]{:S(2)}, u32[]{:S(2)}) collective-permute-start(f32[81,2,256]{2,1,0:T(2,128)S(1)} %get-tuple-element.129), channel_id=1, source_target_pairs={{1,0},{2,1},{3,2},{4,3},{5,4},{6,5},{7,6},{9,8},{10,9},{11,10},{12... | collective-permute-start | bytes 497672 | tf_op jit(solution)/shard_map/ppermute | solution.py:31
  8.0 0.7 convert_element_type.19
  8.7 2.4 %plan.1 = (s32[48,256]{1,0:T(8,128)S(1)}, s32[48,256]{1,0:T(8,128)S(1)}, s32[16,256]{1,0:T(8,128)S(1)}, f32[48,256]{1,0:T(8,128)S(1)}, f32[48,256]{1,0:T(8,128)S...) custom-call(s32[64,256]{1,0:T(8,128)} %mask_ref.1, f32[64,256]{1,0:T(8,128)} %u_ref.1, ...), custom_call_target="tpu_custom_call" | custom-call | tf_op jit(solution)/shard_map/plan/pallas_call | solution.py:207
  11.8 0.1 pad_add_fusion
  11.8 0.0 collective-permute-done
  11.8 0.0 collective-permute-done.1
  11.9 141.7 %conditional.1 = (f32[81,64,256]{2,1,0:T(8,128)}) conditional(s32[]{:T(128)} %bitcast.8, (s32[]{:T(128)}, f32[36,8]{0,1:T(8,128)}, f32[2,36]{1,0:T(2,128)}, f32[81,64,256]{2,1,0:T(8,128)}, f32[81,2,256]{2,1,0:T(2,128)S(1)}, /*index=5*/f32[81,2,256]{2,1,0:T(2,128)S(1)}, s32[64,256]{1,0:T(8,128)}, s32[64,256]{1,0:T(8,128)}, f32[64]{0:T(128)S(1)}, ...), branch_computations={%region_0.1_spmd, %region_1.2_spmd} | conditional | flops 1 | bytes 35532192 | solution.py:609
  11.9 12.7 %propagate.3 = f32[7808,128]{1,0:T(8,128)S(1)} custom-call(s32[1]{0:T(128)} %bitcast.4.refs_0_, f32[2,36]{1,0:T(2,128)} %get-tuple-element.92.refs_1_, f32[8,36]{1,0:T(8,128)} %bitcast.16, s32[13]{0:T(128)S(1)} %get-tuple-element.94.refs_3_, f32[81,64,256]{2,1,0:T(8,128)} %get-tuple-element.95.refs_4_, f32[81,2,256]{2,1,0:T(2,128)S(1)} %get-tuple-element.96.refs_5_, ...), custom_call_target="tpu_custom_call" | custom-call | tf_op jit(solution)/shard_map/cond/branch_1_fun/propagate/pallas_call | solution.py:373
  24.6 0.0 copy-start.1
  24.6 0.0 copy-start.7
  24.6 58.5 %all_to_all.18.wire_ref = f32[16,488,128]{2,1,0:T(8,128)S(1)} all-to-all(f32[16,488,128]{2,1,0:T(8,128)S(1)} %bitcast.13), channel_id=1, replica_groups=mesh['comp'=16,'space'=8] {'comp'}, dimensions={0} | all-to-all | bytes 7995392 | tf_op jit(solution)/shard_map/cond/branch_1_fun/all_to_all | solution.py:585
  83.1 0.0 copy-done.1
  83.1 0.0 copy-done.7
  83.1 11.0 %source.3 = f32[16,488,128]{2,1,0:T(8,128)S(1)} custom-call(s32[2]{0:T(128)S(1)} %get-tuple-element.90.spot_ref, f32[16,488,128]{2,1,0:T(8,128)S(1)} %all_to_all.18.wire_ref, f32[48,256]{1,0:T(8,128)S(1)} %get-tuple-element.102.east_ref, f32[48,256]{1,0:T(8,128)S(1)} %get-tuple-element.103.north_ref, f32[48,256]{1,0:T(8,128)S(1)} %get-tuple-element.104.turn_ref, ...), custom_call_target="tpu_custom_call" | custom-call | tf_op jit(solution)/shard_map/cond/branch_1_fun/source/pallas_call | solution.py:497
  94.2 0.0 copy-start.3
  94.2 55.2 %all_to_all.19 = f32[16,488,128]{2,1,0:T(8,128)S(1)} all-to-all(f32[16,488,128]{2,1,0:T(8,128)S(1)} %source.3), channel_id=1, replica_groups=mesh['comp'=16,'space'=8] {'comp'}, dimensions={0} | all-to-all | bytes 7995392 | tf_op jit(solution)/shard_map/cond/branch_1_fun/all_to_all | solution.py:585
  149.4 0.0 copy-done.3
  149.4 3.9 %unpack.3 = f32[81,64,256]{2,1,0:T(8,128)} custom-call(s32[4]{0:T(128)S(1)} %get-tuple-element.89.refs_0_, f32[7808,128]{1,0:T(8,128)S(1)} %bitcast.14, s32[64,256]{1,0:T(8,128)S(1)} %copy-done.3, s32[16,256]{1,0:T(8,128)S(1)} %get-tuple-element.107.refs_3_), custom_call_target="tpu_custom_call" | custom-call | tf_op jit(solution)/shard_map/cond/branch_1_fun/unpack/pallas_call | solution.py:572
  (1 shorter events, 0.0 us)
Async XLA Ops:
  2.4 9.4 %collective-permute-start = (f32[81,2,256]{2,1,0:T(2,128)S(1)}, f32[81,2,256]{2,1,0:T(2,128)S(1)}, u32[]{:S(2)}, u32[]{:S(2)}) collective-permute-start(f32[81,2,256]{2,1,0:T(2,128)S(1)} %get-tuple-element.130), channel_id=1, source_target_pairs={{0,1},{1,2},{2,3},{3,4},{4,5},{5,6},{6,7},{8,9},{9,10},{10,11},{11... | collective-permute-start | bytes 497672 | tf_op jit(solution)/shard_map/ppermute | solution.py:30
  4.4 7.5 %collective-permute-start.1 = (f32[81,2,256]{2,1,0:T(2,128)S(1)}, f32[81,2,256]{2,1,0:T(2,128)S(1)}, u32[]{:S(2)}, u32[]{:S(2)}) collective-permute-start(f32[81,2,256]{2,1,0:T(2,128)S(1)} %get-tuple-element.129), channel_id=1, source_target_pairs={{1,0},{2,1},{3,2},{4,3},{5,4},{6,5},{7,6},{9,8},{10,9},{11,10},{12... | collective-permute-start | bytes 497672 | tf_op jit(solution)/shard_map/ppermute | solution.py:31
  24.6 58.6 %copy-start.1 = (bf16[1296,1296]{1,0:T(8,128)(2,1)S(1)}, bf16[1296,1296]{1,0:T(8,128)(2,1)}, u32[]{:S(2)}) copy-start(bf16[1296,1296]{1,0:T(8,128)(2,1)} %get-tuple-element.105.coupling_ref) | copy-start | bytes 10077700 | tf_op jit(solution)/shard_map/cond
  24.6 58.6 %copy-start.7 = (f32[72,8]{1,0:T(8,128)S(1)}, f32[72,8]{1,0:T(8,128)}, u32[]{:S(2)}) copy-start(f32[72,8]{1,0:T(8,128)} %get-tuple-element.106.dir_ref) | copy-start | bytes 6916 | tf_op jit(solution)/shard_map/cond
  94.2 55.3 %copy-start.3 = (s32[64,256]{1,0:T(8,128)S(1)}, s32[64,256]{1,0:T(8,128)}, u32[]{:S(2)}) copy-start(s32[64,256]{1,0:T(8,128)} %get-tuple-element.98.refs_7_.refs_2_) | copy-start | bytes 196612 | tf_op jit(solution)/shard_map/cond

commit v4 on v3

--- a/solution.py
+++ b/solution.py
@@ -254,14 +254,14 @@
     def body(*refs):
         refs = list(refs)
         first_ref, turn_ref, speed_ref = refs[:3]
-        flag_ref = refs[3] if packed else None
-        refs = refs[3 + packed:]
+        flag_ref, left_ref = refs[3:5] if packed else (None, None)
+        refs = refs[3 + 2 * packed:]
         spec_ref = refs[0]
         below_ref, above_ref = refs[1:3] if edged else (None, None)
         refs = refs[1 + 2 * edged:]
         mask_ref, depth_ref = refs[:2]
         fill_ref, spare_ref = refs[2:4] if packed else (None, None)
-        out_ref, base_ref, sea_ref, pad_ref, field_ref = refs[2 + 2 * packed:]
+        out_ref, base_ref, sea_ref, pad_ref, field_ref, one_ref, two_ref = refs[2 + 2 * packed:]
         step = pl.program_id(0)
         start = first_ref[0] + step * run
         f = start // ND
@@ -282,10 +282,20 @@
 
         lane = lax.broadcasted_iota(jnp.int32, (SUBS, LANES), 1)
 
-        def sweep(centre, near, far, amount):
-            one = amount * (2.0 - amount)
-            two = 0.5 * (amount - one)
+        def sweep(centre, near, far, one, two):
             return centre + one * (near - centre) + two * (far - centre)
+
+        def factors(cc, carry):
+            wide = turn_ref[0, start % ND + cc]
+            for t in tiles:
+                place = pl.ds(t * SUBS, SUBS)
+                amount = base_ref[place, :] * wide
+                one = amount * (2.0 - amount)
+                one_ref[cc, place, :] = one
+                two_ref[cc, place, :] = 0.5 * (amount - one)
+            return carry
+
+        lax.fori_loop(0, run, factors, 0, unroll=3)
 
         def shifted(parts, by):
             turned = [pltpu.roll(part, by % LANES, 1) for part in parts]
@@ -297,9 +307,6 @@
 
         def run_all(sign_x, sign_y):
             def component(cc, carry):
-                d = start % ND + cc
-                wide_x = turn_ref[0, d]
-                wide_y = turn_ref[1, d]
                 needed = sorted({n for t in tiles for n in (t, t - sign_x) if 0 <= n < layout.tiles})
                 if edged:
                     pad_ref[cc, pl.ds(SUBS - 2, 2), :] = below_ref[step * run + cc]
@@ -310,18 +317,17 @@
                 for t in tiles:
                     place = pl.ds(t * SUBS, SUBS)
                     at = (t + 1) * SUBS
-                    base = base_ref[place, :]
                     centre = pad_ref[cc, pl.ds(at, SUBS), :]
                     near = pad_ref[cc, pl.ds(at - sign_x, SUBS), :]
                     far = pad_ref[cc, pl.ds(at - 2 * sign_x, SUBS), :]
-                    centre = sweep(centre, near, far, base * wide_x) * sea_ref[place, :]
-                    amount = base * wide_y
+                    centre = sweep(centre, near, far, one_ref[cc, place, :], two_ref[cc, place, :]) * sea_ref[place, :]
                     parts = [centre[:, h * LANES:(h + 1) * LANES] for h in range(layout.halves)]
                     near = shifted(parts, sign_y)
                     far = shifted(parts, 2 * sign_y)
                     for h in range(layout.halves):
                         lanes = slice(h * LANES, (h + 1) * LANES)
-                        field_ref[cc, place, lanes] = sweep(parts[h], near[h], far[h], amount[:, lanes])
+                        one, two = one_ref[run - 1 - cc, place, lanes], two_ref[run - 1 - cc, place, lanes]
+                        field_ref[cc, place, lanes] = sweep(parts[h], near[h], far[h], one, two)
                 return carry
 
             lax.fori_loop(0, run, component, 0, unroll=9)
@@ -346,40 +352,38 @@
         if not packed:
             return
 
-        def fill_spare(b):
+        def fill_spare(b, j):
             t, h = layout.blocks[b]
             spare = view(spare_ref, t, h)
             for cc in range(run):
-                value = base_value(t, h, cc)
-                for j, guest in enumerate(layout.guests):
-                    if j != layout.guest_of(t, h):
-                        other = take_lanes(view(field_ref.at[cc], *guest), spare & (LANES - 1))
-                        value = jnp.where(spare >> 7 == j, other, value)
-                put(t, h, cc, value)
+                lines = wire.lines(t, h, step * run + cc)
+                other = take_lanes(view(field_ref.at[cc], *layout.guests[j]), spare & (LANES - 1))
+                out_ref[lines, :] = jnp.where(spare >> 7 == j, other, out_ref[lines, :])
 
         @pl.when(flag_ref[len(layout.blocks)] > 0)
         def _():
             for b in wire.blocks:
-                pl.when(flag_ref[b] >= 0)(lambda b=b: fill_spare(b))
+                for j in range(len(layout.guests)):
+                    if j != layout.guest_of(*layout.blocks[b]):
+                        pl.when((flag_ref[b] >= 0) & (left_ref[j] != 0))(lambda b=b, j=j: fill_spare(b, j))
 
     smem = pl.BlockSpec(memory_space=pltpu.SMEM)
 
-    def fixed(array):
-        return pl.BlockSpec(array.shape, lambda i: (0,) * array.ndim)
-
-    extra_smem = [filling[2]] if packed else []
+    extra_smem = list(filling[2:]) if packed else []
     extra = list(filling[:2]) if packed else []
     shape = (wire.groups * wire.pitch, LANES)
     out = pl.pallas_call(
         body,
         grid=(steps,),
-        in_specs=[smem] * (3 + len(extra_smem)) + [pl.BlockSpec((run, rows, columns), lambda i: (i, 0, 0))] + [fixed(edge) for edge in edges] + [fixed(mask), fixed(depth_level)] + [fixed(a) for a in extra],
+        in_specs=[smem] * (3 + len(extra_smem)) + [pl.BlockSpec((run, rows, columns), lambda i: (i, 0, 0))] + [VMEM_SPEC] * (len(edges) + 2 + len(extra)),
         out_specs=VMEM_SPEC,
         out_shape=jax.ShapeDtypeStruct(shape, jnp.float32),
         scratch_shapes=[
             pltpu.VMEM((rows, columns), jnp.float32),
             pltpu.VMEM((rows, columns), jnp.float32),
             pltpu.VMEM((run, rows + 2 * SUBS, columns), jnp.float32),
+            pltpu.VMEM((run, rows, columns), jnp.float32),
+            pltpu.VMEM((run, rows, columns), jnp.float32),
             pltpu.VMEM((run, rows, columns), jnp.float32),
         ],
         compiler_params=pltpu.CompilerParams(vmem_limit_bytes=24 * MIB, dimension_semantics=("arbitrary",)),
@@ -522,6 +526,7 @@
     def body(*refs):
         refs = list(refs)
         flag_ref = refs.pop(0) if packed else None
+        spare_flag = refs.pop(0) if packed else None
         wire_refs = [refs.pop(0) for _ in wires]
         mask_ref = refs.pop(0)
         back_ref = refs.pop(0) if packed else None
@@ -545,6 +550,14 @@
                     value = jnp.where(back >> 7 == b, found, value)
                 out_ref[(cc,) + place] = value
 
+        def fetch_spare(j, b):
+            t, h = layout.guests[j]
+            place = (pl.ds(t * SUBS, SUBS), pl.ds(h * LANES, LANES))
+            back = view(back_ref, layout.guest_tiles.index(t), h)
+            for cc in range(run):
+                found = take_lanes(get(*layout.blocks[b], cc), back & (LANES - 1))
+                out_ref[(cc,) + place] = jnp.where(back >> 7 == b, found, out_ref[(cc,) + place])
+
         for i, h in layout.blocks:
             place = (pl.ds(layout.hosts[i] * SUBS, SUBS), pl.ds(h * LANES, LANES))
             sea = mask_ref[place] > 0
@@ -553,7 +566,11 @@
         for j in range(len(layout.guests)):
             fetch(j, [b for b, at in enumerate(layout.blocks) if layout.guest_of(*at) == j])
         for j in range(len(layout.guests)):
-            pl.when(flag_ref[j] != 0)(lambda j=j: fetch(j, range(len(layout.blocks))))
+            @pl.when(flag_ref[j] != 0)
+            def _():
+                for b, at in enumerate(layout.blocks):
+                    if layout.guest_of(*at) != j:
+                        pl.when(spare_flag[b] >= 0)(lambda b=b: fetch_spare(j, b))
 
         def send(at):
             place = pl.ds(at * run, run)
@@ -567,7 +584,7 @@
                 send(at).wait()
 
     smem = pl.BlockSpec(memory_space=pltpu.SMEM)
-    extra_smem = [back[1]] if packed else []
+    extra_smem = list(back[1:]) if packed else []
     inputs = [array.reshape(-1, LANES) for array in arrays] + [mask] + ([back[0]] if packed else [])
     return pl.pallas_call(
         body,
@@ -608,7 +625,7 @@
     every = jnp.broadcast_to(substeps.astype(jnp.float32)[:, None], mask.shape)
     return lax.cond(
         fits[0] > 0,
-        lambda: step(hosts, guests, (fill, spare, flag), east, north, turns, (back, back_flag)),
+        lambda: step(hosts, guests, (fill, spare, flag, back_flag), east, north, turns, (back, back_flag, flag)),
         lambda: step(list(range(tiles)), [], None, wind_u, wind_v, every, None),
     )
 

time: 155 us -> 153 us (0.987)
  blocking collectives: 114 us -> 112 us
    all_to_all x2, blocking collectives: 114 us -> 112 us  [regroup(): return lax.all_to_all(wire, 'comp', split_axis=0, concat_axis=0, tiled=True)]
where the time goes in v4:
time: 153 us
  blocking collectives  112 us (73%)
  Pallas kernels  30.9 us (20%)
  starting transfers between devices  5.56 us (4%)
  local copies, waits for them, and re-layouts  2.28 us (1%)
    all_to_all x2, blocking collectives, regroup(): return lax.all_to_all(wire, 'comp', split_axis=0, concat_axis=0, tiled=True)  112 us
    pallas_call x1, Pallas kernels, apply_source(): pl.pallas_call(body, grid=(pairs,), in_specs=[SMEM_SPEC] + [VMEM_SPEC] *...  12.4 us
    pallas_call x1, Pallas kernels, propagate(): pl.pallas_call(body, grid=(steps,), in_specs=[smem] * (3 + len(extra_smem...  12.2 us
    pallas_call x1, Pallas kernels, unpack(): pl.pallas_call(body, grid=(steps,), in_specs=[smem] * len(extra_smem) + [...  3.92 us
    ppermute x1, starting transfers between devices, edge_rows(): above = lax.ppermute(head, axis, [(i + 1, i) for i in range(ends)])  3.64 us
  transfers between devices with their start and end apart: 2, of which 0 were waited for; matrix products, arithmetic and copies ran while one was open for 0% of the time, Pallas kernels for 2%

profile of v4, /device:TPU:32, one launch (start us, length us, event | category | flops | bytes accessed | tf_op | source)
XLA Modules:
  0.0 152.6 jit_solution(14702471006666206538)
XLA Ops:
  0.0 0.7 fusion.2
  0.7 1.4 fusion
  2.1 0.2 maximum_multiply_fusion
  2.3 0.1 fusion.1
  2.4 1.9 %collective-permute-start = (f32[81,2,256]{2,1,0:T(2,128)S(1)}, f32[81,2,256]{2,1,0:T(2,128)S(1)}, u32[]{:S(2)}, u32[]{:S(2)}) collective-permute-start(f32[81,2,256]{2,1,0:T(2,128)S(1)} %get-tuple-element.130), channel_id=1, source_target_pairs={{0,1},{1,2},{2,3},{3,4},{4,5},{5,6},{6,7},{8,9},{9,10},{10,11},{11... | collective-permute-start | bytes 497672 | tf_op jit(solution)/shard_map/ppermute | solution.py:30
  4.4 3.6 %collective-permute-start.1 = (f32[81,2,256]{2,1,0:T(2,128)S(1)}, f32[81,2,256]{2,1,0:T(2,128)S(1)}, u32[]{:S(2)}, u32[]{:S(2)}) collective-permute-start(f32[81,2,256]{2,1,0:T(2,128)S(1)} %get-tuple-element.129), channel_id=1, source_target_pairs={{1,0},{2,1},{3,2},{4,3},{5,4},{6,5},{7,6},{9,8},{10,9},{11,10},{12... | collective-permute-start | bytes 497672 | tf_op jit(solution)/shard_map/ppermute | solution.py:31
  8.0 0.7 convert_element_type.19
  8.7 2.4 %plan.1 = (s32[48,256]{1,0:T(8,128)S(1)}, s32[48,256]{1,0:T(8,128)S(1)}, s32[16,256]{1,0:T(8,128)S(1)}, f32[48,256]{1,0:T(8,128)S(1)}, f32[48,256]{1,0:T(8,128)S...) custom-call(s32[64,256]{1,0:T(8,128)} %mask_ref.1, f32[64,256]{1,0:T(8,128)} %u_ref.1, ...), custom_call_target="tpu_custom_call" | custom-call | tf_op jit(solution)/shard_map/plan/pallas_call | solution.py:207
  11.8 0.1 pad_add_fusion
  11.8 0.0 collective-permute-done
  11.8 0.0 collective-permute-done.1
  11.9 140.6 %conditional.1 = (f32[81,64,256]{2,1,0:T(8,128)}) conditional(s32[]{:T(128)} %bitcast.8, (s32[]{:T(128)}, f32[36,8]{0,1:T(8,128)}, f32[2,36]{1,0:T(2,128)}, f32[81,64,256]{2,1,0:T(8,128)}, f32[81,2,256]{2,1,0:T(2,128)S(1)}, /*index=5*/f32[81,2,256]{2,1,0:T(2,128)S(1)}, s32[64,256]{1,0:T(8,128)}, s32[64,256]{1,0:T(8,128)}, f32[64]{0:T(128)S(1)}, ...), branch_computations={%region_0.1_spmd, %region_1.2_spmd} | conditional | flops 1 | bytes 35532192 | solution.py:626
  11.9 12.2 %propagate.3 = f32[7808,128]{1,0:T(8,128)S(1)} custom-call(s32[1]{0:T(128)} %bitcast.4.refs_0_, f32[2,36]{1,0:T(2,128)} %get-tuple-element.93.refs_1_, f32[8,36]{1,0:T(8,128)} %bitcast.16, s32[13]{0:T(128)S(1)} %get-tuple-element.90.refs_3_.refs_1_, s32[4]{0:T(128)S(1)} %get-tuple-element.89.refs_4_.refs_0_, f32[81,64,256]{2,1,0:T(8,128)} %get-tuple-element.95.refs_5_, ...), custom_call_target="tpu_custom_call" | custom-call | tf_op jit(solution)/shard_map/cond/branch_1_fun/propagate/pallas_call | solution.py:375
  24.1 0.0 copy-start.1
  24.1 0.0 copy-start.7
  24.1 58.5 %all_to_all.18.wire_ref = f32[16,488,128]{2,1,0:T(8,128)S(1)} all-to-all(f32[16,488,128]{2,1,0:T(8,128)S(1)} %bitcast.13), channel_id=1, replica_groups=mesh['comp'=16,'space'=8] {'comp'}, dimensions={0} | all-to-all | bytes 7995392 | tf_op jit(solution)/shard_map/cond/branch_1_fun/all_to_all | solution.py:602
  82.6 0.0 copy-done.1
  82.6 0.0 copy-done.7
  82.6 12.4 %source.3 = f32[16,488,128]{2,1,0:T(8,128)S(1)} custom-call(s32[2]{0:T(128)S(1)} %get-tuple-element.91.spot_ref, f32[16,488,128]{2,1,0:T(8,128)S(1)} %all_to_all.18.wire_ref, f32[48,256]{1,0:T(8,128)S(1)} %get-tuple-element.102.east_ref, f32[48,256]{1,0:T(8,128)S(1)} %get-tuple-element.103.north_ref, f32[48,256]{1,0:T(8,128)S(1)} %get-tuple-element.104.turn_ref, ...), custom_call_target="tpu_custom_call" | custom-call | tf_op jit(solution)/shard_map/cond/branch_1_fun/source/pallas_call | solution.py:501
  95.0 0.0 copy-start.3
  95.0 53.2 %all_to_all.19 = f32[16,488,128]{2,1,0:T(8,128)S(1)} all-to-all(f32[16,488,128]{2,1,0:T(8,128)S(1)} %source.3), channel_id=1, replica_groups=mesh['comp'=16,'space'=8] {'comp'}, dimensions={0} | all-to-all | bytes 7995392 | tf_op jit(solution)/shard_map/cond/branch_1_fun/all_to_all | solution.py:602
  148.3 0.0 copy-done.3
  148.3 3.9 %unpack.3 = f32[81,64,256]{2,1,0:T(8,128)} custom-call(s32[4]{0:T(128)S(1)} %get-tuple-element.89.refs_4_.refs_0_, s32[13]{0:T(128)S(1)} %get-tuple-element.90.refs_3_.refs_1_, f32[7808,128]{1,0:T(8,128)S(1)} %bitcast.14, s32[64,256]{1,0:T(8,128)S(1)} %copy-done.3, s32[16,256]{1,0:T(8,128)S(1)} %get-tuple-element.107.refs_4_), custom_call_target="tpu_custom_call" | custom-call | tf_op jit(solution)/shard_map/cond/branch_1_fun/unpack/pallas_call | solution.py:589
  (1 shorter events, 0.0 us)
Async XLA Ops:
  2.4 9.4 %collective-permute-start = (f32[81,2,256]{2,1,0:T(2,128)S(1)}, f32[81,2,256]{2,1,0:T(2,128)S(1)}, u32[]{:S(2)}, u32[]{:S(2)}) collective-permute-start(f32[81,2,256]{2,1,0:T(2,128)S(1)} %get-tuple-element.130), channel_id=1, source_target_pairs={{0,1},{1,2},{2,3},{3,4},{4,5},{5,6},{6,7},{8,9},{9,10},{10,11},{11... | collective-permute-start | bytes 497672 | tf_op jit(solution)/shard_map/ppermute | solution.py:30
  4.4 7.5 %collective-permute-start.1 = (f32[81,2,256]{2,1,0:T(2,128)S(1)}, f32[81,2,256]{2,1,0:T(2,128)S(1)}, u32[]{:S(2)}, u32[]{:S(2)}) collective-permute-start(f32[81,2,256]{2,1,0:T(2,128)S(1)} %get-tuple-element.129), channel_id=1, source_target_pairs={{1,0},{2,1},{3,2},{4,3},{5,4},{6,5},{7,6},{9,8},{10,9},{11,10},{12... | collective-permute-start | bytes 497672 | tf_op jit(solution)/shard_map/ppermute | solution.py:31
  24.1 58.6 %copy-start.1 = (bf16[1296,1296]{1,0:T(8,128)(2,1)S(1)}, bf16[1296,1296]{1,0:T(8,128)(2,1)}, u32[]{:S(2)}) copy-start(bf16[1296,1296]{1,0:T(8,128)(2,1)} %get-tuple-element.105.coupling_ref) | copy-start | bytes 10077700 | tf_op jit(solution)/shard_map/cond
  24.1 58.5 %copy-start.7 = (f32[72,8]{1,0:T(8,128)S(1)}, f32[72,8]{1,0:T(8,128)}, u32[]{:S(2)}) copy-start(f32[72,8]{1,0:T(8,128)} %get-tuple-element.106.dir_ref) | copy-start | bytes 6916 | tf_op jit(solution)/shard_map/cond
  95.0 53.3 %copy-start.3 = (s32[64,256]{1,0:T(8,128)S(1)}, s32[64,256]{1,0:T(8,128)}, u32[]{:S(2)}) copy-start(s32[64,256]{1,0:T(8,128)} %get-tuple-element.98.refs_8_.refs_3_) | copy-start | bytes 196612 | tf_op jit(solution)/shard_map/cond
